TPU v7x, 32 devices: a whole 2x2x4 slice. The times are simulated.
32 devices in a mesh: gx: 8 (over y, x, core), gy: 4 (over z).
Axes of the slice: x: 2, y: 2, z: 4, core: 2. Of those that a mesh axis runs over, the one named last changes fastest.
Arguments:
- elevation: float32 [8, 128, 1024], P(None, 'gy', 'gx'), may hold values from -4 to 4
- east_velocity: float32 [8, 128, 1024], P(None, 'gy', 'gx'), may hold values from -3 to 3
- north_velocity: float32 [8, 128, 1024], P(None, 'gy', 'gx'), may hold values from -3 to 3
- water_depth: float32 [128, 1024], P('gy', 'gx'), may hold values from 0.3 to 1
- land_sea: int32 [128, 1024], P('gy', 'gx'), may hold values 0 or 1
Outputs:
- surface: float32 [8, 128, 1024], P(None, 'gy', 'gx')
- east_flow: float32 [8, 128, 1024], P(None, 'gy', 'gx')
- north_flow: float32 [8, 128, 1024], P(None, 'gy', 'gx')
- loading: float32 [8, 16, 128], P(None, 'gy', 'gx')
All inputs are finite; a program needn't handle non-finite values. No bound on the sum of `land_sea` on one device may be relied on, other than what follows from the above.
Results may differ from a plain program's by a relative error of at most 0.0032.
Values may be sent and summed in bfloat16 or wider, within the bound.
A program may use at most 64 MiB of HBM per device.

v0:
```python
import math

import jax
import jax.numpy as jnp
from jax import lax
from jax.sharding import PartitionSpec as P

STEPS = 4
INTERVALS = 2
BLOCK = 8


COURANT = 0.35
FRICTION = 0.02
CORIOLIS = 0.3
GREEN_SCALE = 0.25


def with_halo(shard, sides, width, wrap):
    for axis, dim in sides:
        devices, length = (lax.axis_size(axis), shard.shape[dim])
        up = [(i, (i + 1) % devices) for i in range(devices if wrap else devices - 1)]
        down = [(j, i) for i, j in up]
        last = lax.slice_in_dim(shard, length - width, length, axis=dim)
        initial = lax.slice_in_dim(shard, 0, width, axis=dim)
        before = lax.ppermute(last, axis, up)
        after = lax.ppermute(initial, axis, down)
        shard = jnp.concatenate([before, shard, after], axis=dim)
    return shard


def latitude(row_ids, row_count):
    return ((row_ids.astype(jnp.float32) + 0.5) / row_count - 0.5) * jnp.pi


def longitude(col_ids, col_count):
    return (col_ids.astype(jnp.float32) + 0.5) / col_count * (2.0 * jnp.pi)


def unit_vectors(lat_angle, lon_angle):
    return (
        jnp.cos(lat_angle) * jnp.cos(lon_angle),
        jnp.cos(lat_angle) * jnp.sin(lon_angle),
        jnp.sin(lat_angle),
    )


def green_block(source, target, coarse_rows):
    first = source[0][:, None] - target[0][None, :]
    second = source[1][:, None] - target[1][None, :]
    third = source[2][:, None] - target[2][None, :]
    chord_len = jnp.sqrt(first * first + second * second + third * third)
    return (GREEN_SCALE / (1.0 + chord_len * (coarse_rows / math.pi))).astype(jnp.bfloat16)


def coarse_loads(height, ocean):
    members, row_total, col_total = height.shape
    blocks = (ocean * height).reshape(members, row_total // BLOCK, BLOCK, col_total // BLOCK, BLOCK)
    return (jnp.sum(blocks, axis=(2, 4)) / BLOCK).astype(jnp.bfloat16)


def refine(loading):
    members, row_blocks, col_blocks = loading.shape
    spread = jnp.broadcast_to(
        loading[:, :, None, :, None], (members, row_blocks, BLOCK, col_blocks, BLOCK)
    )
    return spread.reshape(members, row_blocks * BLOCK, col_blocks * BLOCK)


def velocities(padded, east_now, north_now, ocean, turning):
    grad_east = (padded[:, 1:-1, 2:] - padded[:, 1:-1, :-2]) * 0.5
    grad_north = (padded[:, 2:, 1:-1] - padded[:, :-2, 1:-1]) * 0.5
    east_next = ocean * (east_now + turning * north_now - COURANT * grad_east - FRICTION * east_now)
    north_next = ocean * (
        north_now - turning * east_now - COURANT * grad_north - FRICTION * north_now
    )
    return (east_next, north_next)


def surface_update(height, east_rim, north_rim, ocean):
    outflow = (east_rim[:, :, 2:] - east_rim[:, :, :-2]) * 0.5 + (
        north_rim[:, 2:, :] - north_rim[:, :-2, :]
    ) * 0.5
    return height - ocean * COURANT * outflow


def close_poles(padded, lat_index, lat_devices):
    return close_wide(padded, lat_index, lat_devices, 1)


def close_wide(padded, lat_index, lat_devices, depth):
    total = padded.shape[1]
    row_ids = jnp.arange(total, dtype=jnp.int32)[:, None]
    pole_rows = (row_ids < depth) & (lat_index == 0) | (row_ids >= total - depth) & (
        lat_index == lat_devices - 1
    )
    return jnp.where(pole_rows, 0.0, padded)


def shards(elevation, east_velocity, north_velocity, water_depth, land_sea):
    members, tile_rows, tile_cols = elevation.shape
    lon_devices = lax.axis_size("gx")
    lat_devices = lax.axis_size("gy")
    lon_index = lax.axis_index("gx")
    lat_index = lax.axis_index("gy")
    coarse_rows = tile_rows * lat_devices // BLOCK
    coarse_cols = tile_cols * lon_devices // BLOCK
    rows_here = tile_rows // BLOCK
    cols_here = tile_cols // BLOCK
    per_device = rows_here * cols_here
    ocean = land_sea.astype(jnp.float32)
    fine_rows = lat_index * tile_rows + jnp.arange(tile_rows, dtype=jnp.int32)
    turning = (CORIOLIS * jnp.sin(latitude(fine_rows, tile_rows * lat_devices)))[:, None]
    own_cols = lon_index * cols_here + jnp.arange(cols_here, dtype=jnp.int32)
    target_rows = jnp.repeat(jnp.arange(coarse_rows, dtype=jnp.int32), cols_here)
    target_cols = jnp.tile(own_cols, coarse_rows)

    def locate(flat_index):
        device = flat_index // per_device
        within = flat_index % per_device
        return (
            lat_index * rows_here + within // cols_here,
            device * cols_here + within % cols_here,
        )

    target = unit_vectors(latitude(target_rows, coarse_rows), longitude(target_cols, coarse_cols))
    target_count = target_rows.shape[0]

    def green_rows(first_index, amount):
        src_rows, src_cols = locate(first_index + jnp.arange(amount, dtype=jnp.int32))
        source = unit_vectors(latitude(src_rows, coarse_rows), longitude(src_cols, coarse_cols))
        return green_block(source, target, coarse_rows)

    height, east_now, north_now = (elevation, east_velocity, north_velocity)
    loading = jnp.zeros((members, rows_here, cols_here), jnp.float32)
    for interval in range(INTERVALS):
        block_loads = coarse_loads(height, ocean).reshape(members, per_device)
        zero_sum = jnp.zeros((members, target_count), jnp.float32)
        shard_piece = lax.all_gather(block_loads, "gx", axis=1, tiled=True)
        accumulate_amount = shard_piece.shape[1]
        sub_block = accumulate_amount
        while sub_block > 4096 and sub_block % 2 == 0:
            sub_block = sub_block // 2

        def add_block(block_index, partial_sum):
            offset = block_index * sub_block
            weights = green_rows(offset, sub_block)
            return partial_sum + jnp.dot(shard_piece, weights, preferred_element_type=jnp.float32)

        partial_value = lax.fori_loop(0, accumulate_amount // sub_block, add_block, zero_sum)
        loading = lax.psum_scatter(
            partial_value.reshape(members, coarse_rows, cols_here),
            "gy",
            scatter_dimension=1,
            tiled=True,
        )
        fine_sal = refine(loading)
        for substep in range(STEPS):
            effective = with_halo(height - fine_sal, (("gx", 2), ("gy", 1)), 1, True)
            effective = close_poles(effective, lat_index, lat_devices)
            east_next, north_next = velocities(effective, east_now, north_now, ocean, turning)
            east_rim = with_halo(water_depth * east_next, (("gx", 2),), 1, True)
            north_rim = with_halo(water_depth * north_next, (("gy", 1),), 1, False)
            height = surface_update(height, east_rim, north_rim, ocean)
            east_now, north_now = (east_next, north_next)
    return (height, east_now, north_now, loading)


def solution(mesh):
    in_specs = (
        P(None, "gy", "gx"),
        P(None, "gy", "gx"),
        P(None, "gy", "gx"),
        P("gy", "gx"),
        P("gy", "gx"),
    )
    out_specs = (P(None, "gy", "gx"), P(None, "gy", "gx"), P(None, "gy", "gx"), P(None, "gy", "gx"))
    return jax.shard_map(shards, mesh=mesh, in_specs=in_specs, out_specs=out_specs, check_vma=False)
```

profile of v0, /device:TPU:0, one launch (start us, length us, event | category | flops | bytes accessed | tf_op | source)
XLA Modules:
  0.0 276.8 jit_solution(3573424939269729922)
XLA Ops:
  10.9 10.4 %all-gather = bf16[8,64,8]{1,2,0:T(8,128)(2,1)S(1)} all-gather(bf16[1,64,8]{1,2,0:T(8,128)(2,1)S(1)} %bitcast.16), channel_id=1, replica_groups=mesh['gx'=8,'gy'=4] {'gx'}, dimensions={0}, use_global_device_ids=true | all-gather | bytes 9216 | tf_op jit(solution)/shard_map/all_gather | solution.py:139
  22.7 19.7 %reduce-scatter.3.cloned.1.call-done = f32[8,4,16]{2,0,1:T(8,128)} async-done(((f32[8,16,16]{2,0,1:T(8,128)}), f32[8,4,16]{2,0,1:T(8,128)}) %reduce-scatter.3.cloned.1.call-update) | async-done | bytes 2064 | tf_op jit(solution)/shard_map/reduce_scatter | solution.py:151
  44.7 2.6 collective-permute-start.1
  47.4 2.6 collective-permute-done
  50.2 3.8 %collective-permute-start.3 = (f32[8,1,130]{2,1,0:T(1,128)S(1)}, f32[8,1,130]{2,1,0:T(1,128)S(1)}, u32[]{:S(2)}, u32[]{:S(2)}) collective-permute-start(f32[8,1,130]{2,1,0:T(1,128)S(1)} %get-tuple-element.133), channel_id=1, source_target_pairs={{1,0},{2,1},{3,2},{0,3},{5,4},{6,5},{7,6},{4,7},{9,8},{10,9},{11,1... | collective-permute-start | bytes 12488 | tf_op jit(solution)/shard_map/ppermute | solution.py:27
  57.3 4.5 %collective-permute-start.7 = (f32[8,1,128]{2,1,0:T(1,128)S(1)}, f32[8,1,128]{2,1,0:T(1,128)S(1)}, u32[]{:S(2)}, u32[]{:S(2)}) collective-permute-start(f32[8,1,128]{2,1,0:T(1,128)S(1)} %get-tuple-element.179), channel_id=1, source_target_pairs={{0,1},{1,2},{2,3},{4,5},{5,6},{6,7},{8,9},{9,10},{10,11},{12,13},{... | collective-permute-start | bytes 12296 | tf_op jit(solution)/shard_map/ppermute | solution.py:26
  63.0 3.6 %collective-permute-done.4 = f32[8,32,1]{2,1,0:T(8,128)S(1)} collective-permute-done((f32[8,32,1]{2,1,0:T(8,128)S(1)}, f32[8,32,1]{2,1,0:T(8,128)S(1)}, u32[]{:S(2)}, u32[]{:S(2)}) %collective-permute-start.4) | collective-permute-done | bytes 1056 | tf_op jit(solution)/shard_map/ppermute | solution.py:27
  66.6 1.7 collective-permute-done.5
  68.6 2.6 collective-permute-start.9
  71.3 3.8 %collective-permute-done.8 = f32[8,32,1]{2,1,0:T(8,128)S(1)} collective-permute-done((f32[8,32,1]{2,1,0:T(8,128)S(1)}, f32[8,32,1]{2,1,0:T(8,128)S(1)}, u32[]{:S(2)}, u32[]{:S(2)}) %collective-permute-start.8) | collective-permute-done | bytes 1056 | tf_op jit(solution)/shard_map/ppermute | solution.py:26
  75.5 3.6 %collective-permute-start.11 = (f32[8,1,130]{2,1,0:T(1,128)S(1)}, f32[8,1,130]{2,1,0:T(1,128)S(1)}, u32[]{:S(2)}, u32[]{:S(2)}) collective-permute-start(f32[8,1,130]{2,1,0:T(1,128)S(1)} %get-tuple-element.131), channel_id=1, source_target_pairs={{1,0},{2,1},{3,2},{0,3},{5,4},{6,5},{7,6},{4,7},{9,8},{10,9},{11,1... | collective-permute-start | bytes 12488 | tf_op jit(solution)/shard_map/ppermute | solution.py:27
  82.4 4.5 %collective-permute-start.15 = (f32[8,1,128]{2,1,0:T(1,128)S(1)}, f32[8,1,128]{2,1,0:T(1,128)S(1)}, u32[]{:S(2)}, u32[]{:S(2)}) collective-permute-start(f32[8,1,128]{2,1,0:T(1,128)S(1)} %get-tuple-element.173), channel_id=1, source_target_pairs={{0,1},{1,2},{2,3},{4,5},{5,6},{6,7},{8,9},{9,10},{10,11},{12,13},{... | collective-permute-start | bytes 12296 | tf_op jit(solution)/shard_map/ppermute | solution.py:26
  87.7 3.2 %collective-permute-done.12 = f32[8,32,1]{2,1,0:T(8,128)S(1)} collective-permute-done((f32[8,32,1]{2,1,0:T(8,128)S(1)}, f32[8,32,1]{2,1,0:T(8,128)S(1)}, u32[]{:S(2)}, u32[]{:S(2)}) %collective-permute-start.12) | collective-permute-done | bytes 1056 | tf_op jit(solution)/shard_map/ppermute | solution.py:27
  92.9 2.6 collective-permute-start.17
  95.5 3.1 %collective-permute-done.16 = f32[8,32,1]{2,1,0:T(8,128)S(1)} collective-permute-done((f32[8,32,1]{2,1,0:T(8,128)S(1)}, f32[8,32,1]{2,1,0:T(8,128)S(1)}, u32[]{:S(2)}, u32[]{:S(2)}) %collective-permute-start.16) | collective-permute-done | bytes 1056 | tf_op jit(solution)/shard_map/ppermute | solution.py:26
  99.5 3.1 %collective-permute-start.19 = (f32[8,1,130]{2,1,0:T(1,128)S(1)}, f32[8,1,130]{2,1,0:T(1,128)S(1)}, u32[]{:S(2)}, u32[]{:S(2)}) collective-permute-start(f32[8,1,130]{2,1,0:T(1,128)S(1)} %get-tuple-element.129), channel_id=1, source_target_pairs={{1,0},{2,1},{3,2},{0,3},{5,4},{6,5},{7,6},{4,7},{9,8},{10,9},{11,1... | collective-permute-start | bytes 12488 | tf_op jit(solution)/shard_map/ppermute | solution.py:27
  106.0 4.5 %collective-permute-start.23 = (f32[8,1,128]{2,1,0:T(1,128)S(1)}, f32[8,1,128]{2,1,0:T(1,128)S(1)}, u32[]{:S(2)}, u32[]{:S(2)}) collective-permute-start(f32[8,1,128]{2,1,0:T(1,128)S(1)} %get-tuple-element.167), channel_id=1, source_target_pairs={{0,1},{1,2},{2,3},{4,5},{5,6},{6,7},{8,9},{9,10},{10,11},{12,13},{... | collective-permute-start | bytes 12296 | tf_op jit(solution)/shard_map/ppermute | solution.py:26
  111.2 3.6 %collective-permute-done.20 = f32[8,32,1]{2,1,0:T(8,128)S(1)} collective-permute-done((f32[8,32,1]{2,1,0:T(8,128)S(1)}, f32[8,32,1]{2,1,0:T(8,128)S(1)}, u32[]{:S(2)}, u32[]{:S(2)}) %collective-permute-start.20) | collective-permute-done | bytes 1056 | tf_op jit(solution)/shard_map/ppermute | solution.py:27
  116.8 2.6 collective-permute-start.25
  119.4 2.6 collective-permute-done.24
  122.5 3.5 %collective-permute-start.27 = (f32[8,1,130]{2,1,0:T(1,128)S(1)}, f32[8,1,130]{2,1,0:T(1,128)S(1)}, u32[]{:S(2)}, u32[]{:S(2)}) collective-permute-start(f32[8,1,130]{2,1,0:T(1,128)S(1)} %get-tuple-element.127), channel_id=1, source_target_pairs={{1,0},{2,1},{3,2},{0,3},{5,4},{6,5},{7,6},{4,7},{9,8},{10,9},{11,1... | collective-permute-start | bytes 12488 | tf_op jit(solution)/shard_map/ppermute | solution.py:27
  129.4 4.5 %collective-permute-start.31 = (f32[8,1,128]{2,1,0:T(1,128)S(1)}, f32[8,1,128]{2,1,0:T(1,128)S(1)}, u32[]{:S(2)}, u32[]{:S(2)}) collective-permute-start(f32[8,1,128]{2,1,0:T(1,128)S(1)} %get-tuple-element.161), channel_id=1, source_target_pairs={{0,1},{1,2},{2,3},{4,5},{5,6},{6,7},{8,9},{9,10},{10,11},{12,13},{... | collective-permute-start | bytes 12296 | tf_op jit(solution)/shard_map/ppermute | solution.py:26
  135.0 2.9 %collective-permute-done.28 = f32[8,32,1]{2,1,0:T(8,128)S(1)} collective-permute-done((f32[8,32,1]{2,1,0:T(8,128)S(1)}, f32[8,32,1]{2,1,0:T(8,128)S(1)}, u32[]{:S(2)}, u32[]{:S(2)}) %collective-permute-start.28) | collective-permute-done | bytes 1056 | tf_op jit(solution)/shard_map/ppermute | solution.py:27
  138.0 2.3 collective-permute-done.29
  142.0 9.6 %all-gather.1 = bf16[8,64,8]{1,2,0:T(8,128)(2,1)S(1)} all-gather(bf16[1,64,8]{1,2,0:T(8,128)(2,1)S(1)} %bitcast.17), channel_id=1, replica_groups=mesh['gx'=8,'gy'=4] {'gx'}, dimensions={0}, use_global_device_ids=true | all-gather | bytes 9216 | tf_op jit(solution)/shard_map/all_gather | solution.py:139
  153.0 17.8 %reduce-scatter.5.cloned.1.call-done = f32[8,4,16]{2,0,1:T(8,128)} async-done(((f32[8,16,16]{2,0,1:T(8,128)}), f32[8,4,16]{2,0,1:T(8,128)}) %reduce-scatter.5.cloned.1.call-update) | async-done | bytes 2064 | tf_op jit(solution)/shard_map/reduce_scatter | solution.py:151
  173.0 2.6 collective-permute-start.33
  175.6 2.6 collective-permute-done.32
  178.5 3.8 %collective-permute-start.35 = (f32[8,1,130]{2,1,0:T(1,128)S(1)}, f32[8,1,130]{2,1,0:T(1,128)S(1)}, u32[]{:S(2)}, u32[]{:S(2)}) collective-permute-start(f32[8,1,130]{2,1,0:T(1,128)S(1)} %get-tuple-element.125), channel_id=1, source_target_pairs={{1,0},{2,1},{3,2},{0,3},{5,4},{6,5},{7,6},{4,7},{9,8},{10,9},{11,1... | collective-permute-start | bytes 12488 | tf_op jit(solution)/shard_map/ppermute | solution.py:27
  185.6 4.5 %collective-permute-start.39 = (f32[8,1,128]{2,1,0:T(1,128)S(1)}, f32[8,1,128]{2,1,0:T(1,128)S(1)}, u32[]{:S(2)}, u32[]{:S(2)}) collective-permute-start(f32[8,1,128]{2,1,0:T(1,128)S(1)} %get-tuple-element.155), channel_id=1, source_target_pairs={{0,1},{1,2},{2,3},{4,5},{5,6},{6,7},{8,9},{9,10},{10,11},{12,13},{... | collective-permute-start | bytes 12296 | tf_op jit(solution)/shard_map/ppermute | solution.py:26
  191.2 3.6 %collective-permute-done.36 = f32[8,32,1]{2,1,0:T(8,128)S(1)} collective-permute-done((f32[8,32,1]{2,1,0:T(8,128)S(1)}, f32[8,32,1]{2,1,0:T(8,128)S(1)}, u32[]{:S(2)}, u32[]{:S(2)}) %collective-permute-start.36) | collective-permute-done | bytes 1056 | tf_op jit(solution)/shard_map/ppermute | solution.py:27
  196.9 2.6 collective-permute-start.41
  199.5 3.6 %collective-permute-done.40 = f32[8,32,1]{2,1,0:T(8,128)S(1)} collective-permute-done((f32[8,32,1]{2,1,0:T(8,128)S(1)}, f32[8,32,1]{2,1,0:T(8,128)S(1)}, u32[]{:S(2)}, u32[]{:S(2)}) %collective-permute-start.40) | collective-permute-done | bytes 1056 | tf_op jit(solution)/shard_map/ppermute | solution.py:26
  203.9 3.3 %collective-permute-start.43 = (f32[8,1,130]{2,1,0:T(1,128)S(1)}, f32[8,1,130]{2,1,0:T(1,128)S(1)}, u32[]{:S(2)}, u32[]{:S(2)}) collective-permute-start(f32[8,1,130]{2,1,0:T(1,128)S(1)} %get-tuple-element.123), channel_id=1, source_target_pairs={{1,0},{2,1},{3,2},{0,3},{5,4},{6,5},{7,6},{4,7},{9,8},{10,9},{11,1... | collective-permute-start | bytes 12488 | tf_op jit(solution)/shard_map/ppermute | solution.py:27
  210.5 4.5 %collective-permute-start.47 = (f32[8,1,128]{2,1,0:T(1,128)S(1)}, f32[8,1,128]{2,1,0:T(1,128)S(1)}, u32[]{:S(2)}, u32[]{:S(2)}) collective-permute-start(f32[8,1,128]{2,1,0:T(1,128)S(1)} %get-tuple-element.149), channel_id=1, source_target_pairs={{0,1},{1,2},{2,3},{4,5},{5,6},{6,7},{8,9},{9,10},{10,11},{12,13},{... | collective-permute-start | bytes 12296 | tf_op jit(solution)/shard_map/ppermute | solution.py:26
  215.8 3.2 %collective-permute-done.44 = f32[8,32,1]{2,1,0:T(8,128)S(1)} collective-permute-done((f32[8,32,1]{2,1,0:T(8,128)S(1)}, f32[8,32,1]{2,1,0:T(8,128)S(1)}, u32[]{:S(2)}, u32[]{:S(2)}) %collective-permute-start.44) | collective-permute-done | bytes 1056 | tf_op jit(solution)/shard_map/ppermute | solution.py:27
  221.0 2.6 collective-permute-start.49
  223.6 2.9 %collective-permute-done.48 = f32[8,32,1]{2,1,0:T(8,128)S(1)} collective-permute-done((f32[8,32,1]{2,1,0:T(8,128)S(1)}, f32[8,32,1]{2,1,0:T(8,128)S(1)}, u32[]{:S(2)}, u32[]{:S(2)}) %collective-permute-start.48) | collective-permute-done | bytes 1056 | tf_op jit(solution)/shard_map/ppermute | solution.py:26
  227.3 3.1 %collective-permute-start.51 = (f32[8,1,130]{2,1,0:T(1,128)S(1)}, f32[8,1,130]{2,1,0:T(1,128)S(1)}, u32[]{:S(2)}, u32[]{:S(2)}) collective-permute-start(f32[8,1,130]{2,1,0:T(1,128)S(1)} %get-tuple-element.121), channel_id=1, source_target_pairs={{1,0},{2,1},{3,2},{0,3},{5,4},{6,5},{7,6},{4,7},{9,8},{10,9},{11,1... | collective-permute-start | bytes 12488 | tf_op jit(solution)/shard_map/ppermute | solution.py:27
  233.9 4.5 %collective-permute-start.55 = (f32[8,1,128]{2,1,0:T(1,128)S(1)}, f32[8,1,128]{2,1,0:T(1,128)S(1)}, u32[]{:S(2)}, u32[]{:S(2)}) collective-permute-start(f32[8,1,128]{2,1,0:T(1,128)S(1)} %get-tuple-element.143), channel_id=1, source_target_pairs={{0,1},{1,2},{2,3},{4,5},{5,6},{6,7},{8,9},{9,10},{10,11},{12,13},{... | collective-permute-start | bytes 12296 | tf_op jit(solution)/shard_map/ppermute | solution.py:26
  239.2 3.5 %collective-permute-done.52 = f32[8,32,1]{2,1,0:T(8,128)S(1)} collective-permute-done((f32[8,32,1]{2,1,0:T(8,128)S(1)}, f32[8,32,1]{2,1,0:T(8,128)S(1)}, u32[]{:S(2)}, u32[]{:S(2)}) %collective-permute-start.52) | collective-permute-done | bytes 1056 | tf_op jit(solution)/shard_map/ppermute | solution.py:27
  242.7 1.8 collective-permute-done.53
  244.9 2.6 collective-permute-start.57
  247.5 2.6 collective-permute-done.56
  250.6 3.5 %collective-permute-start.59 = (f32[8,1,130]{2,1,0:T(1,128)S(1)}, f32[8,1,130]{2,1,0:T(1,128)S(1)}, u32[]{:S(2)}, u32[]{:S(2)}) collective-permute-start(f32[8,1,130]{2,1,0:T(1,128)S(1)} %get-tuple-element.119), channel_id=1, source_target_pairs={{1,0},{2,1},{3,2},{0,3},{5,4},{6,5},{7,6},{4,7},{9,8},{10,9},{11,1... | collective-permute-start | bytes 12488 | tf_op jit(solution)/shard_map/ppermute | solution.py:27
  258.2 4.5 %collective-permute-start.63 = (f32[8,1,128]{2,1,0:T(1,128)S(1)}, f32[8,1,128]{2,1,0:T(1,128)S(1)}, u32[]{:S(2)}, u32[]{:S(2)}) collective-permute-start(f32[8,1,128]{2,1,0:T(1,128)S(1)} %get-tuple-element.137), channel_id=1, source_target_pairs={{0,1},{1,2},{2,3},{4,5},{5,6},{6,7},{8,9},{9,10},{10,11},{12,13},{... | collective-permute-start | bytes 12296 | tf_op jit(solution)/shard_map/ppermute | solution.py:26
  263.8 2.8 %collective-permute-done.60 = f32[8,32,1]{2,1,0:T(8,128)S(1)} collective-permute-done((f32[8,32,1]{2,1,0:T(8,128)S(1)}, f32[8,32,1]{2,1,0:T(8,128)S(1)}, u32[]{:S(2)}, u32[]{:S(2)}) %collective-permute-start.60) | collective-permute-done | bytes 1056 | tf_op jit(solution)/shard_map/ppermute | solution.py:27
  266.6 2.5 collective-permute-done.61
  (196 shorter events, 60.5 us)
Async XLA Ops:
  7.2 35.3 %reduce-scatter.3.cloned.1.call-start = ((), (), s32[]{:S(2)}) async-start(), calls=%async_computation.2 | async-start | bytes 81920 | tf_op jit(solution)/shard_map/reduce_scatter | solution.py:151
  22.7 148.1 %reduce-scatter.5.cloned.1.call-start = ((), (), s32[]{:S(2)}) async-start(), calls=%async_computation.3 | async-start | bytes 81920 | tf_op jit(solution)/shard_map/reduce_scatter | solution.py:151
  44.6 5.3 %collective-permute-start = (f32[8,32,1]{2,1,0:T(8,128)S(1)}, f32[8,32,1]{2,1,0:T(8,128)S(1)}, u32[]{:S(2)}, u32[]{:S(2)}) collective-permute-start(f32[8,32,1]{2,1,0:T(8,128)S(1)} %get-tuple-element.180), channel_id=1, source_target_pairs={{0,4},{4,8},{8,12},{12,16},{16,20},{20,24},{24,28},{28,0},{1,5},{5... | collective-permute-start | bytes 3080 | tf_op jit(solution)/shard_map/ppermute | solution.py:26
  50.1 5.5 %collective-permute-start.2 = (f32[8,1,130]{2,1,0:T(1,128)S(1)}, f32[8,1,130]{2,1,0:T(1,128)S(1)}, u32[]{:S(2)}, u32[]{:S(2)}) collective-permute-start(f32[8,1,130]{2,1,0:T(1,128)S(1)} %get-tuple-element.132), channel_id=1, source_target_pairs={{0,1},{1,2},{2,3},{3,0},{4,5},{5,6},{6,7},{7,4},{8,9},{9,10},{10,1... | collective-permute-start | bytes 12488 | tf_op jit(solution)/shard_map/ppermute | solution.py:26
  50.2 5.4 %collective-permute-start.3 = (f32[8,1,130]{2,1,0:T(1,128)S(1)}, f32[8,1,130]{2,1,0:T(1,128)S(1)}, u32[]{:S(2)}, u32[]{:S(2)}) collective-permute-start(f32[8,1,130]{2,1,0:T(1,128)S(1)} %get-tuple-element.133), channel_id=1, source_target_pairs={{1,0},{2,1},{3,2},{0,3},{5,4},{6,5},{7,6},{4,7},{9,8},{10,9},{11,1... | collective-permute-start | bytes 12488 | tf_op jit(solution)/shard_map/ppermute | solution.py:27
  56.0 12.2 %collective-permute-start.6 = (f32[8,1,128]{2,1,0:T(1,128)S(1)}, f32[8,1,128]{2,1,0:T(1,128)S(1)}, u32[]{:S(2)}, u32[]{:S(2)}) collective-permute-start(f32[8,1,128]{2,1,0:T(1,128)S(1)} %get-tuple-element.178), channel_id=1, source_target_pairs={{1,0},{2,1},{3,2},{5,4},{6,5},{7,6},{9,8},{10,9},{11,10},{13,12},{... | collective-permute-start | bytes 12296 | tf_op jit(solution)/shard_map/ppermute | solution.py:27
  57.3 10.9 %collective-permute-start.7 = (f32[8,1,128]{2,1,0:T(1,128)S(1)}, f32[8,1,128]{2,1,0:T(1,128)S(1)}, u32[]{:S(2)}, u32[]{:S(2)}) collective-permute-start(f32[8,1,128]{2,1,0:T(1,128)S(1)} %get-tuple-element.179), channel_id=1, source_target_pairs={{0,1},{1,2},{2,3},{4,5},{5,6},{6,7},{8,9},{9,10},{10,11},{12,13},{... | collective-permute-start | bytes 12296 | tf_op jit(solution)/shard_map/ppermute | solution.py:26
  63.0 5.3 %collective-permute-start.5 = (f32[8,32,1]{2,1,0:T(8,128)S(1)}, f32[8,32,1]{2,1,0:T(8,128)S(1)}, u32[]{:S(2)}, u32[]{:S(2)}) collective-permute-start(f32[8,32,1]{2,1,0:T(8,128)S(1)} %get-tuple-element.177), channel_id=1, source_target_pairs={{0,4},{4,8},{8,12},{12,16},{16,20},{20,24},{24,28},{28,0},{1,5},{5... | collective-permute-start | bytes 3080 | tf_op jit(solution)/shard_map/ppermute | solution.py:26
  68.6 6.5 %collective-permute-start.8 = (f32[8,32,1]{2,1,0:T(8,128)S(1)}, f32[8,32,1]{2,1,0:T(8,128)S(1)}, u32[]{:S(2)}, u32[]{:S(2)}) collective-permute-start(f32[8,32,1]{2,1,0:T(8,128)S(1)} %get-tuple-element.174), channel_id=1, source_target_pairs={{0,4},{4,8},{8,12},{12,16},{16,20},{20,24},{24,28},{28,0},{1,5},{5... | collective-permute-start | bytes 3080 | tf_op jit(solution)/shard_map/ppermute | solution.py:26
  68.6 6.4 %collective-permute-start.9 = (f32[8,32,1]{2,1,0:T(8,128)S(1)}, f32[8,32,1]{2,1,0:T(8,128)S(1)}, u32[]{:S(2)}, u32[]{:S(2)}) collective-permute-start(f32[8,32,1]{2,1,0:T(8,128)S(1)} %get-tuple-element.175), channel_id=1, source_target_pairs={{4,0},{8,4},{12,8},{16,12},{20,16},{24,20},{28,24},{0,28},{5,1},{9... | collective-permute-start | bytes 3080 | tf_op jit(solution)/shard_map/ppermute | solution.py:27
  75.2 5.5 %collective-permute-start.10 = (f32[8,1,130]{2,1,0:T(1,128)S(1)}, f32[8,1,130]{2,1,0:T(1,128)S(1)}, u32[]{:S(2)}, u32[]{:S(2)}) collective-permute-start(f32[8,1,130]{2,1,0:T(1,128)S(1)} %get-tuple-element.130), channel_id=1, source_target_pairs={{0,1},{1,2},{2,3},{3,0},{4,5},{5,6},{6,7},{7,4},{8,9},{9,10},{10,1... | collective-permute-start | bytes 12488 | tf_op jit(solution)/shard_map/ppermute | solution.py:26
  81.1 11.4 %collective-permute-start.14 = (f32[8,1,128]{2,1,0:T(1,128)S(1)}, f32[8,1,128]{2,1,0:T(1,128)S(1)}, u32[]{:S(2)}, u32[]{:S(2)}) collective-permute-start(f32[8,1,128]{2,1,0:T(1,128)S(1)} %get-tuple-element.172), channel_id=1, source_target_pairs={{1,0},{2,1},{3,2},{5,4},{6,5},{7,6},{9,8},{10,9},{11,10},{13,12},{... | collective-permute-start | bytes 12296 | tf_op jit(solution)/shard_map/ppermute | solution.py:27
  82.4 10.1 %collective-permute-start.15 = (f32[8,1,128]{2,1,0:T(1,128)S(1)}, f32[8,1,128]{2,1,0:T(1,128)S(1)}, u32[]{:S(2)}, u32[]{:S(2)}) collective-permute-start(f32[8,1,128]{2,1,0:T(1,128)S(1)} %get-tuple-element.173), channel_id=1, source_target_pairs={{0,1},{1,2},{2,3},{4,5},{5,6},{6,7},{8,9},{9,10},{10,11},{12,13},{... | collective-permute-start | bytes 12296 | tf_op jit(solution)/shard_map/ppermute | solution.py:26
  87.2 5.3 %collective-permute-start.13 = (f32[8,32,1]{2,1,0:T(8,128)S(1)}, f32[8,32,1]{2,1,0:T(8,128)S(1)}, u32[]{:S(2)}, u32[]{:S(2)}) collective-permute-start(f32[8,32,1]{2,1,0:T(8,128)S(1)} %get-tuple-element.171), channel_id=1, source_target_pairs={{0,4},{4,8},{8,12},{12,16},{16,20},{20,24},{24,28},{28,0},{1,5},{5... | collective-permute-start | bytes 3080 | tf_op jit(solution)/shard_map/ppermute | solution.py:26
  92.8 5.8 %collective-permute-start.16 = (f32[8,32,1]{2,1,0:T(8,128)S(1)}, f32[8,32,1]{2,1,0:T(8,128)S(1)}, u32[]{:S(2)}, u32[]{:S(2)}) collective-permute-start(f32[8,32,1]{2,1,0:T(8,128)S(1)} %get-tuple-element.168), channel_id=1, source_target_pairs={{0,4},{4,8},{8,12},{12,16},{16,20},{20,24},{24,28},{28,0},{1,5},{5... | collective-permute-start | bytes 3080 | tf_op jit(solution)/shard_map/ppermute | solution.py:26
  92.9 5.7 %collective-permute-start.17 = (f32[8,32,1]{2,1,0:T(8,128)S(1)}, f32[8,32,1]{2,1,0:T(8,128)S(1)}, u32[]{:S(2)}, u32[]{:S(2)}) collective-permute-start(f32[8,32,1]{2,1,0:T(8,128)S(1)} %get-tuple-element.169), channel_id=1, source_target_pairs={{4,0},{8,4},{12,8},{16,12},{20,16},{24,20},{28,24},{0,28},{5,1},{9... | collective-permute-start | bytes 3080 | tf_op jit(solution)/shard_map/ppermute | solution.py:27
  98.7 5.6 %collective-permute-start.18 = (f32[8,1,130]{2,1,0:T(1,128)S(1)}, f32[8,1,130]{2,1,0:T(1,128)S(1)}, u32[]{:S(2)}, u32[]{:S(2)}) collective-permute-start(f32[8,1,130]{2,1,0:T(1,128)S(1)} %get-tuple-element.128), channel_id=1, source_target_pairs={{0,1},{1,2},{2,3},{3,0},{4,5},{5,6},{6,7},{7,4},{8,9},{9,10},{10,1... | collective-permute-start | bytes 12488 | tf_op jit(solution)/shard_map/ppermute | solution.py:26
  104.7 11.8 %collective-permute-start.22 = (f32[8,1,128]{2,1,0:T(1,128)S(1)}, f32[8,1,128]{2,1,0:T(1,128)S(1)}, u32[]{:S(2)}, u32[]{:S(2)}) collective-permute-start(f32[8,1,128]{2,1,0:T(1,128)S(1)} %get-tuple-element.166), channel_id=1, source_target_pairs={{1,0},{2,1},{3,2},{5,4},{6,5},{7,6},{9,8},{10,9},{11,10},{13,12},{... | collective-permute-start | bytes 12296 | tf_op jit(solution)/shard_map/ppermute | solution.py:27
  106.0 10.5 %collective-permute-start.23 = (f32[8,1,128]{2,1,0:T(1,128)S(1)}, f32[8,1,128]{2,1,0:T(1,128)S(1)}, u32[]{:S(2)}, u32[]{:S(2)}) collective-permute-start(f32[8,1,128]{2,1,0:T(1,128)S(1)} %get-tuple-element.167), channel_id=1, source_target_pairs={{0,1},{1,2},{2,3},{4,5},{5,6},{6,7},{8,9},{9,10},{10,11},{12,13},{... | collective-permute-start | bytes 12296 | tf_op jit(solution)/shard_map/ppermute | solution.py:26
  111.1 5.3 %collective-permute-start.21 = (f32[8,32,1]{2,1,0:T(8,128)S(1)}, f32[8,32,1]{2,1,0:T(8,128)S(1)}, u32[]{:S(2)}, u32[]{:S(2)}) collective-permute-start(f32[8,32,1]{2,1,0:T(8,128)S(1)} %get-tuple-element.165), channel_id=1, source_target_pairs={{0,4},{4,8},{8,12},{12,16},{16,20},{20,24},{24,28},{28,0},{1,5},{5... | collective-permute-start | bytes 3080 | tf_op jit(solution)/shard_map/ppermute | solution.py:26
  116.7 5.3 %collective-permute-start.24 = (f32[8,32,1]{2,1,0:T(8,128)S(1)}, f32[8,32,1]{2,1,0:T(8,128)S(1)}, u32[]{:S(2)}, u32[]{:S(2)}) collective-permute-start(f32[8,32,1]{2,1,0:T(8,128)S(1)} %get-tuple-element.162), channel_id=1, source_target_pairs={{0,4},{4,8},{8,12},{12,16},{16,20},{20,24},{24,28},{28,0},{1,5},{5... | collective-permute-start | bytes 3080 | tf_op jit(solution)/shard_map/ppermute | solution.py:26
  122.2 5.5 %collective-permute-start.26 = (f32[8,1,130]{2,1,0:T(1,128)S(1)}, f32[8,1,130]{2,1,0:T(1,128)S(1)}, u32[]{:S(2)}, u32[]{:S(2)}) collective-permute-start(f32[8,1,130]{2,1,0:T(1,128)S(1)} %get-tuple-element.126), channel_id=1, source_target_pairs={{0,1},{1,2},{2,3},{3,0},{4,5},{5,6},{6,7},{7,4},{8,9},{9,10},{10,1... | collective-permute-start | bytes 12488 | tf_op jit(solution)/shard_map/ppermute | solution.py:26
  128.1 12.2 %collective-permute-start.30 = (f32[8,1,128]{2,1,0:T(1,128)S(1)}, f32[8,1,128]{2,1,0:T(1,128)S(1)}, u32[]{:S(2)}, u32[]{:S(2)}) collective-permute-start(f32[8,1,128]{2,1,0:T(1,128)S(1)} %get-tuple-element.160), channel_id=1, source_target_pairs={{1,0},{2,1},{3,2},{5,4},{6,5},{7,6},{9,8},{10,9},{11,10},{13,12},{... | collective-permute-start | bytes 12296 | tf_op jit(solution)/shard_map/ppermute | solution.py:27
  129.4 10.9 %collective-permute-start.31 = (f32[8,1,128]{2,1,0:T(1,128)S(1)}, f32[8,1,128]{2,1,0:T(1,128)S(1)}, u32[]{:S(2)}, u32[]{:S(2)}) collective-permute-start(f32[8,1,128]{2,1,0:T(1,128)S(1)} %get-tuple-element.161), channel_id=1, source_target_pairs={{0,1},{1,2},{2,3},{4,5},{5,6},{6,7},{8,9},{9,10},{10,11},{12,13},{... | collective-permute-start | bytes 12296 | tf_op jit(solution)/shard_map/ppermute | solution.py:26
  135.0 5.3 %collective-permute-start.29 = (f32[8,32,1]{2,1,0:T(8,128)S(1)}, f32[8,32,1]{2,1,0:T(8,128)S(1)}, u32[]{:S(2)}, u32[]{:S(2)}) collective-permute-start(f32[8,32,1]{2,1,0:T(8,128)S(1)} %get-tuple-element.159), channel_id=1, source_target_pairs={{0,4},{4,8},{8,12},{12,16},{16,20},{20,24},{24,28},{28,0},{1,5},{5... | collective-permute-start | bytes 3080 | tf_op jit(solution)/shard_map/ppermute | solution.py:26
  172.9 5.3 %collective-permute-start.32 = (f32[8,32,1]{2,1,0:T(8,128)S(1)}, f32[8,32,1]{2,1,0:T(8,128)S(1)}, u32[]{:S(2)}, u32[]{:S(2)}) collective-permute-start(f32[8,32,1]{2,1,0:T(8,128)S(1)} %get-tuple-element.156), channel_id=1, source_target_pairs={{0,4},{4,8},{8,12},{12,16},{16,20},{20,24},{24,28},{28,0},{1,5},{5... | collective-permute-start | bytes 3080 | tf_op jit(solution)/shard_map/ppermute | solution.py:26
  178.4 5.5 %collective-permute-start.34 = (f32[8,1,130]{2,1,0:T(1,128)S(1)}, f32[8,1,130]{2,1,0:T(1,128)S(1)}, u32[]{:S(2)}, u32[]{:S(2)}) collective-permute-start(f32[8,1,130]{2,1,0:T(1,128)S(1)} %get-tuple-element.124), channel_id=1, source_target_pairs={{0,1},{1,2},{2,3},{3,0},{4,5},{5,6},{6,7},{7,4},{8,9},{9,10},{10,1... | collective-permute-start | bytes 12488 | tf_op jit(solution)/shard_map/ppermute | solution.py:26
  178.5 5.4 %collective-permute-start.35 = (f32[8,1,130]{2,1,0:T(1,128)S(1)}, f32[8,1,130]{2,1,0:T(1,128)S(1)}, u32[]{:S(2)}, u32[]{:S(2)}) collective-permute-start(f32[8,1,130]{2,1,0:T(1,128)S(1)} %get-tuple-element.125), channel_id=1, source_target_pairs={{1,0},{2,1},{3,2},{0,3},{5,4},{6,5},{7,6},{4,7},{9,8},{10,9},{11,1... | collective-permute-start | bytes 12488 | tf_op jit(solution)/shard_map/ppermute | solution.py:27
  184.3 12.2 %collective-permute-start.38 = (f32[8,1,128]{2,1,0:T(1,128)S(1)}, f32[8,1,128]{2,1,0:T(1,128)S(1)}, u32[]{:S(2)}, u32[]{:S(2)}) collective-permute-start(f32[8,1,128]{2,1,0:T(1,128)S(1)} %get-tuple-element.154), channel_id=1, source_target_pairs={{1,0},{2,1},{3,2},{5,4},{6,5},{7,6},{9,8},{10,9},{11,10},{13,12},{... | collective-permute-start | bytes 12296 | tf_op jit(solution)/shard_map/ppermute | solution.py:27
  185.6 10.9 %collective-permute-start.39 = (f32[8,1,128]{2,1,0:T(1,128)S(1)}, f32[8,1,128]{2,1,0:T(1,128)S(1)}, u32[]{:S(2)}, u32[]{:S(2)}) collective-permute-start(f32[8,1,128]{2,1,0:T(1,128)S(1)} %get-tuple-element.155), channel_id=1, source_target_pairs={{0,1},{1,2},{2,3},{4,5},{5,6},{6,7},{8,9},{9,10},{10,11},{12,13},{... | collective-permute-start | bytes 12296 | tf_op jit(solution)/shard_map/ppermute | solution.py:26
  191.2 5.3 %collective-permute-start.37 = (f32[8,32,1]{2,1,0:T(8,128)S(1)}, f32[8,32,1]{2,1,0:T(8,128)S(1)}, u32[]{:S(2)}, u32[]{:S(2)}) collective-permute-start(f32[8,32,1]{2,1,0:T(8,128)S(1)} %get-tuple-element.153), channel_id=1, source_target_pairs={{0,4},{4,8},{8,12},{12,16},{16,20},{20,24},{24,28},{28,0},{1,5},{5... | collective-permute-start | bytes 3080 | tf_op jit(solution)/shard_map/ppermute | solution.py:26
  196.8 6.3 %collective-permute-start.40 = (f32[8,32,1]{2,1,0:T(8,128)S(1)}, f32[8,32,1]{2,1,0:T(8,128)S(1)}, u32[]{:S(2)}, u32[]{:S(2)}) collective-permute-start(f32[8,32,1]{2,1,0:T(8,128)S(1)} %get-tuple-element.150), channel_id=1, source_target_pairs={{0,4},{4,8},{8,12},{12,16},{16,20},{20,24},{24,28},{28,0},{1,5},{5... | collective-permute-start | bytes 3080 | tf_op jit(solution)/shard_map/ppermute | solution.py:26
  196.9 6.3 %collective-permute-start.41 = (f32[8,32,1]{2,1,0:T(8,128)S(1)}, f32[8,32,1]{2,1,0:T(8,128)S(1)}, u32[]{:S(2)}, u32[]{:S(2)}) collective-permute-start(f32[8,32,1]{2,1,0:T(8,128)S(1)} %get-tuple-element.151), channel_id=1, source_target_pairs={{4,0},{8,4},{12,8},{16,12},{20,16},{24,20},{28,24},{0,28},{5,1},{9... | collective-permute-start | bytes 3080 | tf_op jit(solution)/shard_map/ppermute | solution.py:27
  203.3 5.5 %collective-permute-start.42 = (f32[8,1,130]{2,1,0:T(1,128)S(1)}, f32[8,1,130]{2,1,0:T(1,128)S(1)}, u32[]{:S(2)}, u32[]{:S(2)}) collective-permute-start(f32[8,1,130]{2,1,0:T(1,128)S(1)} %get-tuple-element.122), channel_id=1, source_target_pairs={{0,1},{1,2},{2,3},{3,0},{4,5},{5,6},{6,7},{7,4},{8,9},{9,10},{10,1... | collective-permute-start | bytes 12488 | tf_op jit(solution)/shard_map/ppermute | solution.py:26
  209.2 11.4 %collective-permute-start.46 = (f32[8,1,128]{2,1,0:T(1,128)S(1)}, f32[8,1,128]{2,1,0:T(1,128)S(1)}, u32[]{:S(2)}, u32[]{:S(2)}) collective-permute-start(f32[8,1,128]{2,1,0:T(1,128)S(1)} %get-tuple-element.148), channel_id=1, source_target_pairs={{1,0},{2,1},{3,2},{5,4},{6,5},{7,6},{9,8},{10,9},{11,10},{13,12},{... | collective-permute-start | bytes 12296 | tf_op jit(solution)/shard_map/ppermute | solution.py:27
  210.5 10.1 %collective-permute-start.47 = (f32[8,1,128]{2,1,0:T(1,128)S(1)}, f32[8,1,128]{2,1,0:T(1,128)S(1)}, u32[]{:S(2)}, u32[]{:S(2)}) collective-permute-start(f32[8,1,128]{2,1,0:T(1,128)S(1)} %get-tuple-element.149), channel_id=1, source_target_pairs={{0,1},{1,2},{2,3},{4,5},{5,6},{6,7},{8,9},{9,10},{10,11},{12,13},{... | collective-permute-start | bytes 12296 | tf_op jit(solution)/shard_map/ppermute | solution.py:26
  215.3 5.3 %collective-permute-start.45 = (f32[8,32,1]{2,1,0:T(8,128)S(1)}, f32[8,32,1]{2,1,0:T(8,128)S(1)}, u32[]{:S(2)}, u32[]{:S(2)}) collective-permute-start(f32[8,32,1]{2,1,0:T(8,128)S(1)} %get-tuple-element.147), channel_id=1, source_target_pairs={{0,4},{4,8},{8,12},{12,16},{16,20},{20,24},{24,28},{28,0},{1,5},{5... | collective-permute-start | bytes 3080 | tf_op jit(solution)/shard_map/ppermute | solution.py:26
  220.9 5.6 %collective-permute-start.48 = (f32[8,32,1]{2,1,0:T(8,128)S(1)}, f32[8,32,1]{2,1,0:T(8,128)S(1)}, u32[]{:S(2)}, u32[]{:S(2)}) collective-permute-start(f32[8,32,1]{2,1,0:T(8,128)S(1)} %get-tuple-element.144), channel_id=1, source_target_pairs={{0,4},{4,8},{8,12},{12,16},{16,20},{20,24},{24,28},{28,0},{1,5},{5... | collective-permute-start | bytes 3080 | tf_op jit(solution)/shard_map/ppermute | solution.py:26
  221.0 5.5 %collective-permute-start.49 = (f32[8,32,1]{2,1,0:T(8,128)S(1)}, f32[8,32,1]{2,1,0:T(8,128)S(1)}, u32[]{:S(2)}, u32[]{:S(2)}) collective-permute-start(f32[8,32,1]{2,1,0:T(8,128)S(1)} %get-tuple-element.145), channel_id=1, source_target_pairs={{4,0},{8,4},{12,8},{16,12},{20,16},{24,20},{28,24},{0,28},{5,1},{9... | collective-permute-start | bytes 3080 | tf_op jit(solution)/shard_map/ppermute | solution.py:27
  226.6 5.6 %collective-permute-start.50 = (f32[8,1,130]{2,1,0:T(1,128)S(1)}, f32[8,1,130]{2,1,0:T(1,128)S(1)}, u32[]{:S(2)}, u32[]{:S(2)}) collective-permute-start(f32[8,1,130]{2,1,0:T(1,128)S(1)} %get-tuple-element.120), channel_id=1, source_target_pairs={{0,1},{1,2},{2,3},{3,0},{4,5},{5,6},{6,7},{7,4},{8,9},{9,10},{10,1... | collective-permute-start | bytes 12488 | tf_op jit(solution)/shard_map/ppermute | solution.py:26
  232.6 11.9 %collective-permute-start.54 = (f32[8,1,128]{2,1,0:T(1,128)S(1)}, f32[8,1,128]{2,1,0:T(1,128)S(1)}, u32[]{:S(2)}, u32[]{:S(2)}) collective-permute-start(f32[8,1,128]{2,1,0:T(1,128)S(1)} %get-tuple-element.142), channel_id=1, source_target_pairs={{1,0},{2,1},{3,2},{5,4},{6,5},{7,6},{9,8},{10,9},{11,10},{13,12},{... | collective-permute-start | bytes 12296 | tf_op jit(solution)/shard_map/ppermute | solution.py:27
  233.9 10.6 %collective-permute-start.55 = (f32[8,1,128]{2,1,0:T(1,128)S(1)}, f32[8,1,128]{2,1,0:T(1,128)S(1)}, u32[]{:S(2)}, u32[]{:S(2)}) collective-permute-start(f32[8,1,128]{2,1,0:T(1,128)S(1)} %get-tuple-element.143), channel_id=1, source_target_pairs={{0,1},{1,2},{2,3},{4,5},{5,6},{6,7},{8,9},{9,10},{10,11},{12,13},{... | collective-permute-start | bytes 12296 | tf_op jit(solution)/shard_map/ppermute | solution.py:26
  239.2 5.3 %collective-permute-start.53 = (f32[8,32,1]{2,1,0:T(8,128)S(1)}, f32[8,32,1]{2,1,0:T(8,128)S(1)}, u32[]{:S(2)}, u32[]{:S(2)}) collective-permute-start(f32[8,32,1]{2,1,0:T(8,128)S(1)} %get-tuple-element.141), channel_id=1, source_target_pairs={{0,4},{4,8},{8,12},{12,16},{16,20},{20,24},{24,28},{28,0},{1,5},{5... | collective-permute-start | bytes 3080 | tf_op jit(solution)/shard_map/ppermute | solution.py:26
  244.8 5.3 %collective-permute-start.56 = (f32[8,32,1]{2,1,0:T(8,128)S(1)}, f32[8,32,1]{2,1,0:T(8,128)S(1)}, u32[]{:S(2)}, u32[]{:S(2)}) collective-permute-start(f32[8,32,1]{2,1,0:T(8,128)S(1)} %get-tuple-element.138), channel_id=1, source_target_pairs={{0,4},{4,8},{8,12},{12,16},{16,20},{20,24},{24,28},{28,0},{1,5},{5... | collective-permute-start | bytes 3080 | tf_op jit(solution)/shard_map/ppermute | solution.py:26
  250.3 5.5 %collective-permute-start.58 = (f32[8,1,130]{2,1,0:T(1,128)S(1)}, f32[8,1,130]{2,1,0:T(1,128)S(1)}, u32[]{:S(2)}, u32[]{:S(2)}) collective-permute-start(f32[8,1,130]{2,1,0:T(1,128)S(1)} %get-tuple-element.118), channel_id=1, source_target_pairs={{0,1},{1,2},{2,3},{3,0},{4,5},{5,6},{6,7},{7,4},{8,9},{9,10},{10,1... | collective-permute-start | bytes 12488 | tf_op jit(solution)/shard_map/ppermute | solution.py:26
  256.9 12.2 %collective-permute-start.62 = (f32[8,1,128]{2,1,0:T(1,128)S(1)}, f32[8,1,128]{2,1,0:T(1,128)S(1)}, u32[]{:S(2)}, u32[]{:S(2)}) collective-permute-start(f32[8,1,128]{2,1,0:T(1,128)S(1)} %get-tuple-element.136), channel_id=1, source_target_pairs={{1,0},{2,1},{3,2},{5,4},{6,5},{7,6},{9,8},{10,9},{11,10},{13,12},{... | collective-permute-start | bytes 12296 | tf_op jit(solution)/shard_map/ppermute | solution.py:27
  258.2 10.9 %collective-permute-start.63 = (f32[8,1,128]{2,1,0:T(1,128)S(1)}, f32[8,1,128]{2,1,0:T(1,128)S(1)}, u32[]{:S(2)}, u32[]{:S(2)}) collective-permute-start(f32[8,1,128]{2,1,0:T(1,128)S(1)} %get-tuple-element.137), channel_id=1, source_target_pairs={{0,1},{1,2},{2,3},{4,5},{5,6},{6,7},{8,9},{9,10},{10,11},{12,13},{... | collective-permute-start | bytes 12296 | tf_op jit(solution)/shard_map/ppermute | solution.py:26
  263.8 5.3 %collective-permute-start.61 = (f32[8,32,1]{2,1,0:T(8,128)S(1)}, f32[8,32,1]{2,1,0:T(8,128)S(1)}, u32[]{:S(2)}, u32[]{:S(2)}) collective-permute-start(f32[8,32,1]{2,1,0:T(8,128)S(1)} %get-tuple-element.135), channel_id=1, source_target_pairs={{0,4},{4,8},{8,12},{12,16},{16,20},{20,24},{24,28},{28,0},{1,5},{5... | collective-permute-start | bytes 3080 | tf_op jit(solution)/shard_map/ppermute | solution.py:26
  (24 other events, 142.2 us)
Sparse Core Ops, SparseCore 0:
  22.8 19.6 reduce-scatter.2
  153.1 17.6 reduce-scatter.4
where the time goes:
time: 278 us; the launch traced here: 277 us
  waiting for transfers between devices  116 us (42%)
  starting transfers between devices  106 us (38%)
  blocking collectives  20 us (7%)
  between operations  14.8 us (5%)
  local copies, waits for them, and re-layouts  9.84 us (4%)
  other arithmetic  9.35 us (3%)
    ppermute x32, starting transfers between devices, with_halo(): after = lax.ppermute(initial, axis, down)  64.3 us
    ppermute x32, waiting for transfers between devices, with_halo(): before = lax.ppermute(last, axis, up)  52.2 us
    ppermute x32, starting transfers between devices, with_halo(): before = lax.ppermute(last, axis, up)  41.1 us
    reduce_scatter x2, waiting for transfers between devices, shards(): lax.psum_scatter(partial_value.reshape(members, coarse_rows, cols_here),...  37.6 us
    ppermute x32, waiting for transfers between devices, with_halo(): after = lax.ppermute(initial, axis, down)  26.4 us
    all_gather x2, blocking collectives, shards(): shard_piece = lax.all_gather(block_loads, 'gx', axis=1, tiled=True)  20 us
  transfers between devices with their start and end apart: 66, of which 34 were waited for; matrix products, arithmetic and copies ran while one was open for 0% of the time, Pallas kernels for 0%

commit v1 on v0

v1 whole, which is shorter than its diff:
```python
import functools
import math

import jax
import jax.numpy as jnp
from jax import lax
from jax.experimental import pallas as pl
from jax.experimental.pallas import tpu as pltpu
from jax.sharding import PartitionSpec as P

STEPS = 4
INTERVALS = 2
BLOCK = 8
HALO = 2 * STEPS

COURANT = 0.35
FRICTION = 0.02
CORIOLIS = 0.3
GREEN_SCALE = 0.25
CHUNK = 8

MESH = pl.DeviceIdType.MESH
F32 = jnp.float32
BF16 = jnp.bfloat16
DIRS = ((0, 1), (0, -1), (1, 0), (-1, 0), (1, 1), (1, -1), (-1, 1), (-1, -1))


def iota(shape, dim):
    return lax.broadcasted_iota(jnp.int32, shape, dim)


def latitude(row_ids, row_count):
    return ((row_ids.astype(F32) + 0.5) / row_count - 0.5) * jnp.pi


def longitude(col_ids, col_count):
    return (col_ids.astype(F32) + 0.5) / col_count * (2.0 * jnp.pi)


def unit_vectors(lat_angle, lon_angle):
    cos_lat = jnp.cos(lat_angle)
    return (cos_lat * jnp.cos(lon_angle), cos_lat * jnp.sin(lon_angle), jnp.sin(lat_angle))


def split3(x):
    hi = x.astype(BF16).astype(F32)
    rest = x - hi
    mid = rest.astype(BF16).astype(F32)
    return jnp.concatenate([hi, mid, rest - mid], axis=0).astype(BF16)


def exact_dot(x, table):
    rows = x.shape[0]
    out = jnp.dot(split3(x), table, preferred_element_type=F32)
    return out[:rows] + out[rows : 2 * rows] + out[2 * rows :]


def kernel(
    nx, ny, members, rows, cols,
    h_in, u_in, v_in, d_in, o_in,
    h_out, u_out, v_out, l_out,
    in3, in_d, in_o, own, strips, land, slab, st, st_land, st_ns, dmx, turn,
    eta, uu, vv, green, tiles, fine, ind, expand,
    in_sem, gs_sem, gr_sem, hs_sem, hr_sem, ss_sem, sr_sem,
):
    gx, gy = lax.axis_index("gx"), lax.axis_index("gy")
    n = nx * ny
    rb_own, cb_own = rows // BLOCK, cols // BLOCK
    per_device = rb_own * cb_own
    pair_rows = 2 * per_device
    coarse_rows, coarse_cols = rb_own * ny, cb_own * nx
    ext = rows + 2 * HALO
    ext_tiles = ext // BLOCK
    my_slot = ((gx // 2) * ny + gy) * 2 + gx % 2
    lane = iota((members, cols), 1)

    inputs = [
        pltpu.make_async_copy(src, dst, in_sem.at[k])
        for k, (src, dst) in enumerate(
            ((h_in, in3.at[0]), (u_in, in3.at[1]), (v_in, in3.at[2]), (d_in, in_d), (o_in, in_o))
        )
    ]
    for copy in inputs:
        copy.start()

    def partner(offset):
        slot = lax.rem(my_slot + offset, n)
        pair = slot // 2
        return {"gx": (pair // ny) * 2 + slot % 2, "gy": pair % ny}

    barrier = pltpu.get_barrier_semaphore()

    def greet(offset, carry):
        pl.semaphore_signal(barrier, inc=1, device_id=partner(offset), device_id_type=MESH)
        return carry

    lax.fori_loop(1, n, greet, 0)

    def target_of(dx, dy):
        return {"gx": lax.rem(gx + dx + nx, nx), "gy": gy + dy}

    def when(dy, sending, fn):
        if dy == 0:
            fn()
        else:
            beyond = gy + (dy if sending else -dy)
            pl.when((beyond >= 0) & (beyond < ny))(fn)

    def static_copy(k):
        dx, dy = DIRS[k]
        side = 0 if dx > 0 else 1
        if dy == 0:
            src, dst = st, st_land.at[side, pl.ds(HALO, rows)]
        else:
            src = st.at[pl.ds(rows - HALO if dy > 0 else 0, HALO)]
            at = 0 if dy > 0 else HALO + rows
            dst = st_ns.at[0 if dy > 0 else 1] if dx == 0 else st_land.at[side, pl.ds(at, HALO)]
        return pltpu.make_async_remote_copy(
            src_ref=src, dst_ref=dst, send_sem=ss_sem.at[k], recv_sem=sr_sem.at[k],
            device_id=target_of(dx, dy), device_id_type=MESH,
        )

    def halo_copy(i, k):
        dx, dy = DIRS[k]
        side = 0 if dx > 0 else 1
        if dx == 0:
            src = own.at[:, pl.ds(rows - HALO if dy > 0 else 0, HALO)]
            dst = slab.at[i, 0 if dy > 0 else 1]
        elif dy == 0:
            src, dst = strips.at[i], land.at[i, side, :, pl.ds(1, rb_own)]
        else:
            src = strips.at[i, :, pl.ds(rb_own - 1 if dy > 0 else 0, 1)]
            dst = land.at[i, side, :, pl.ds(0 if dy > 0 else ext_tiles - 1, 1)]
        return pltpu.make_async_remote_copy(
            src_ref=src, dst_ref=dst, send_sem=hs_sem.at[i, k], recv_sem=hr_sem.at[i, k],
            device_id=target_of(dx, dy), device_id_type=MESH,
        )

    def clear(side):
        at = 0 if side == 0 else ext_tiles - 1
        slab[:, side] = jnp.zeros_like(slab[:, side])
        land[:, :, :, at] = jnp.zeros_like(land[:, :, :, at])
        st_ns[side] = jnp.zeros_like(st_ns[side])
        st_land[:, at * BLOCK : (at + 1) * BLOCK] = jnp.zeros((2, HALO, cols), F32)

    pl.when(gy == 0)(lambda: clear(0))
    pl.when(gy == ny - 1)(lambda: clear(1))

    k_id = iota((rb_own * cols, pair_rows), 0)
    lane_id = iota((rb_own * cols, pair_rows), 1)
    wanted = (gx % 2) * per_device + (k_id // cols) * cb_own + (k_id % cols) // BLOCK
    ind[...] = jnp.where(wanted == lane_id, 1.0, 0.0).astype(BF16)

    for copy in inputs:
        copy.wait()
    st[...] = jnp.where(in_o[...] > 0, in_d[...], 0.0)
    for k in range(rows):
        for f in range(3):
            own[f, k] = in3[f, pl.ds(k, members, stride=rows), :]

    pl.semaphore_wait(barrier, n - 1)
    for k, (dx, dy) in enumerate(DIRS):
        when(dy, True, lambda k=k: static_copy(k).start())

    def setup():
        t = iota((8, 128), 1)
        north = per_device
        south = north + cb_own
        west = south + cb_own
        east = west + rb_own + 2
        t_row = jnp.where(t < north, t // cb_own, jnp.where(t < south, -1, rb_own))
        t_col = jnp.where(t < north, t % cb_own, jnp.where(t < south, t - north, t - south))
        t_row = jnp.where(t >= east, t - east - 1, jnp.where(t >= west, t - west - 1, t_row))
        t_col = jnp.where(t >= east, cb_own, jnp.where(t >= west, -1, t_col))
        t_row = gy * rb_own + t_row
        t_col = gx * cb_own + t_col
        t_col = jnp.where(t_col < 0, t_col + coarse_cols, t_col)
        t_col = jnp.where(t_col >= coarse_cols, t_col - coarse_cols, t_col)
        target = unit_vectors(latitude(t_row, coarse_rows), longitude(t_col, coarse_cols))
        target = [jnp.broadcast_to(x[:1], (pair_rows, 128)) for x in target]

        def green_group(g, carry):
            p = g * 8 + iota((8, pair_rows), 0)
            k = iota((8, pair_rows), 1)
            s_col = ((p // ny) * 2 + k // per_device) * cb_own + k % cb_own
            s_row = (p % ny) * rb_own + (k % per_device) // cb_own
            source = unit_vectors(latitude(s_row, coarse_rows), longitude(s_col, coarse_cols))
            source = [jnp.transpose(x) for x in source]
            for j in range(8):
                square = None
                for s, t_vec in zip(source, target):
                    diff = jnp.broadcast_to(s[:, j : j + 1], (pair_rows, 128)) - t_vec
                    square = diff * diff if square is None else square + diff * diff
                value = GREEN_SCALE / (1.0 + jnp.sqrt(square) * (coarse_rows / math.pi))
                green[g * 8 + j] = value.astype(BF16)
            return carry

        lax.fori_loop(0, n // 16, green_group, 0)

        t_id = iota((128, 2 * cols), 0)
        l_id = iota((128, 2 * cols), 1)
        for e in range(ext_tiles):
            base = north if e == 0 else south if e == ext_tiles - 1 else (e - 1) * cb_own
            want = jnp.where(
                l_id < cols, base + l_id // BLOCK, jnp.where(l_id < cols + cols // 2, east + e, west + e)
            )
            expand[:, e * 2 * cols : (e + 1) * 2 * cols] = jnp.where(want == t_id, 1.0, 0.0).astype(BF16)

        for e in range(ext_tiles):
            row_ids = gy * rows - HALO + e * BLOCK + iota((BLOCK, cols), 0)
            turning = CORIOLIS * jnp.sin(latitude(row_ids, rows * ny))
            for k in range(BLOCK):
                turn[e * BLOCK + k] = jnp.broadcast_to(turning[k : k + 1], (members, cols))

        for k, (dx, dy) in enumerate(DIRS):
            when(dy, False, lambda k=k: static_copy(k).wait_recv())
            when(dy, True, lambda k=k: static_copy(k).wait_send())
        for e in range(ext_tiles):
            if e == 0:
                main = st_ns[0]
            elif e == ext_tiles - 1:
                main = st_ns[1]
            else:
                main = st[(e - 1) * BLOCK : e * BLOCK]
            part = slice(e * BLOCK, (e + 1) * BLOCK)
            side = jnp.where(iota((BLOCK, cols), 1) < cols // 2, st_land[1, part], st_land[0, part])
            for k in range(BLOCK):
                dmx[e * BLOCK + k, :, :cols] = jnp.broadcast_to(main[k : k + 1], (members, cols))
                dmx[e * BLOCK + k, :, cols:] = jnp.broadcast_to(side[k : k + 1], (members, cols))

    def xdiff(m, a):
        rm, ra = pltpu.roll(m, cols - 1, 1), pltpu.roll(a, cols - 1, 1)
        lm, la = pltpu.roll(m, 1, 1), pltpu.roll(a, 1, 1)
        at_end, at_start = lane == cols - 1, lane == 0
        return (
            jnp.where(at_end, ra, rm) - jnp.where(at_start, la, lm),
            jnp.where(at_end, rm, ra) - jnp.where(at_start, lm, la),
        )

    half = 0.5 * COURANT
    keep = 1.0 - FRICTION

    def sweep(step):
        src, dst = step % 2, 1 - step % 2
        start, count = 1 + 2 * step, ext - 2 - 4 * step

        def pair(ref, r):
            return ref[r, :, :cols], ref[r, :, cols:]

        def one_row(r, carry):
            before, here, north_two, north_one, flow_one = carry
            after = pair(eta.at[src], r + 1)
            u_now, v_now = pair(uu.at[src], r), pair(vv.at[src], r)
            depth, depth_one = pair(dmx, r), pair(dmx, r - 1)
            coriolis = turn[r]
            grad = xdiff(*here)
            du, dv = [], []
            for c in range(2):
                part = slice(c * cols, (c + 1) * cols)
                wet = depth[c] > 0.0
                u_next = keep * u_now[c] + coriolis * v_now[c] - half * grad[c]
                v_next = keep * v_now[c] - coriolis * u_now[c] - half * (after[c] - before[c])
                u_next = jnp.where(wet, u_next, 0.0)
                v_next = jnp.where(wet, v_next, 0.0)
                uu[dst, r, :, part] = u_next
                vv[dst, r, :, part] = v_next
                du.append(depth[c] * u_next)
                dv.append(depth[c] * v_next)
            flow = xdiff(*du)
            for c in range(2):
                part = slice(c * cols, (c + 1) * cols)
                out = half * (flow_one[c] + (dv[c] - north_two[c]))
                eta[dst, r - 1, :, part] = jnp.where(depth_one[c] > 0.0, before[c] - out, before[c])
            return here, after, north_one, tuple(dv), flow

        def chunk(first, amount, carry):
            for k in range(amount):
                carry = one_row(first + k, carry)
            return carry

        zero = jnp.zeros((members, cols), F32)
        zeros = (zero, zero)
        carry = (pair(eta.at[src], start - 1), pair(eta.at[src], start), zeros, zeros, zeros)
        full = count // CHUNK
        carry = lax.fori_loop(0, full, lambda c, x: chunk(start + c * CHUNK, CHUNK, x), carry)
        chunk(start + full * CHUNK, count - full * CHUNK, carry)

    def interval(i, _):
        sums = []
        for b in range(rb_own):
            total = None
            for k in range(BLOCK):
                r = b * BLOCK + k
                mask = jnp.broadcast_to(st[r : r + 1], (members, cols)) > 0.0
                value = jnp.where(mask, own[0, r], 0.0)
                total = value if total is None else total + value
            sums.append(total)
        loads = exact_dot(jnp.concatenate(sums, axis=1), ind[...]) / BLOCK
        tiles[i, my_slot] = loads.astype(BF16)

        def gather_copy(offset):
            return pltpu.make_async_remote_copy(
                src_ref=tiles.at[i, my_slot], dst_ref=tiles.at[i, my_slot],
                send_sem=gs_sem.at[i], recv_sem=gr_sem.at[i],
                device_id=partner(offset), device_id_type=MESH,
            )

        def send(offset, carry):
            gather_copy(offset).start()
            return carry

        lax.fori_loop(1, n, send, 0)
        for k in (0, 1):
            when(DIRS[k][1], True, lambda k=k: halo_copy(i, k).start())

        for f in range(3):
            for b in range(rb_own):
                packed = None
                for k in range(BLOCK):
                    moved = pltpu.roll(own[f, b * BLOCK + k], (HALO + 2 * HALO * k) % cols, 1)
                    packed = moved if packed is None else jnp.where(lane // (2 * HALO) == k, moved, packed)
                strips[i, f, b] = packed
        for k in range(2, len(DIRS)):
            when(DIRS[k][1], True, lambda k=k: halo_copy(i, k).start())

        pl.when(i == 0)(setup)

        everyone = pltpu.make_async_remote_copy(
            src_ref=tiles.at[i, pl.ds(0, n - 1)], dst_ref=tiles.at[i, pl.ds(0, n - 1)],
            send_sem=gs_sem.at[i], recv_sem=gr_sem.at[i],
            device_id=partner(1), device_id_type=MESH,
        )
        everyone.wait_recv()

        group = 16 if n // 2 % 16 == 0 else 1

        def add_group(g, total):
            for j in range(group):
                p = g * group + j
                tile = tiles[i, 2 * p].astype(F32) + tiles[i, 2 * p + 1].astype(F32)
                total = total + jnp.dot(tile.astype(BF16), green[p], preferred_element_type=F32)
            return total

        loading = lax.fori_loop(0, n // 2 // group, add_group, jnp.zeros((members, 128), F32))
        l_out[...] = loading[:, :per_device]
        spread = exact_dot(loading, expand[...])
        for e in range(ext_tiles):
            value = spread[:, e * 2 * cols : (e + 1) * 2 * cols]
            if e == 0:
                value = jnp.where(gy == 0, 0.0, value)
            if e == ext_tiles - 1:
                value = jnp.where(gy == ny - 1, 0.0, value)
            fine[e] = value

        for k, (dx, dy) in enumerate(DIRS):
            when(dy, False, lambda k=k: halo_copy(i, k).wait_recv())
        everyone.wait_send()
        for k, (dx, dy) in enumerate(DIRS):
            when(dy, True, lambda k=k: halo_copy(i, k).wait_send())

        for f, ref in enumerate((eta, uu, vv)):
            for e in range(ext_tiles):
                joined = jnp.where(lane % (2 * HALO) < HALO, land[i, 0, f, e], land[i, 1, f, e])
                for k in range(BLOCK):
                    r = e * BLOCK + k
                    if e == 0:
                        main = slab[i, 0, f, k]
                    elif e == ext_tiles - 1:
                        main = slab[i, 1, f, k]
                    else:
                        main = own[f, r - HALO]
                    side = pltpu.roll(joined, (-(2 * HALO * k + HALO)) % cols, 1)
                    if f == 0:
                        main = main - fine[e, :, :cols]
                        side = side - fine[e, :, cols:]
                    ref[0, r, :, :cols] = main
                    ref[0, r, :, cols:] = side

        for step in range(STEPS):
            sweep(step)
        last = STEPS % 2
        for r in range(rows):
            own[0, r] = eta[last, HALO + r, :, :cols] + fine[1 + r // BLOCK, :, :cols]
            own[1, r] = uu[last, HALO + r, :, :cols]
            own[2, r] = vv[last, HALO + r, :, :cols]
        return 0

    lax.fori_loop(0, INTERVALS, interval, 0)
    for r in range(rows):
        for f, out in enumerate((h_out, u_out, v_out)):
            out[pl.ds(r, members, stride=rows), :] = own[f, r]


def shards(nx, ny, elevation, east_velocity, north_velocity, water_depth, land_sea):
    members, rows, cols = elevation.shape
    rb_own, cb_own = rows // BLOCK, cols // BLOCK
    n = nx * ny
    ext = rows + 2 * HALO
    tiles = ext // BLOCK
    flat = (members * rows, cols)
    any_spec = pl.BlockSpec(memory_space=pl.ANY)
    vmem_spec = pl.BlockSpec(memory_space=pltpu.VMEM)
    dma = pltpu.SemaphoreType.DMA
    field = jax.ShapeDtypeStruct(flat, F32)
    h, u, v, loading = pl.pallas_call(
        functools.partial(kernel, nx, ny, members, rows, cols),
        out_shape=(field, field, field, jax.ShapeDtypeStruct((members, rb_own * cb_own), F32)),
        in_specs=[any_spec] * 5,
        out_specs=(vmem_spec,) * 4,
        scratch_shapes=[
            pltpu.VMEM((3,) + flat, F32),
            pltpu.VMEM((rows, cols), F32),
            pltpu.VMEM((rows, cols), jnp.int32),
            pltpu.VMEM((3, rows, members, cols), F32),
            pltpu.VMEM((INTERVALS, 3, rb_own, members, cols), F32),
            pltpu.VMEM((INTERVALS, 2, 3, tiles, members, cols), F32),
            pltpu.VMEM((INTERVALS, 2, 3, HALO, members, cols), F32),
            pltpu.VMEM((rows, cols), F32),
            pltpu.VMEM((2, ext, cols), F32),
            pltpu.VMEM((2, HALO, cols), F32),
            pltpu.VMEM((ext, members, 2 * cols), F32),
            pltpu.VMEM((ext, members, cols), F32),
            pltpu.VMEM((2, ext, members, 2 * cols), F32),
            pltpu.VMEM((2, ext, members, 2 * cols), F32),
            pltpu.VMEM((2, ext, members, 2 * cols), F32),
            pltpu.VMEM((n // 2, 2 * rb_own * cb_own, 128), BF16),
            pltpu.VMEM((INTERVALS, n, members, 2 * rb_own * cb_own), BF16),
            pltpu.VMEM((tiles, members, 2 * cols), F32),
            pltpu.VMEM((rb_own * cols, 2 * rb_own * cb_own), BF16),
            pltpu.VMEM((128, tiles * 2 * cols), BF16),
            dma((5,)),
            dma((INTERVALS,)),
            dma((INTERVALS,)),
            dma((INTERVALS, len(DIRS))),
            dma((INTERVALS, len(DIRS))),
            dma((len(DIRS),)),
            dma((len(DIRS),)),
        ],
        compiler_params=pltpu.CompilerParams(
            collective_id=0, has_side_effects=True, vmem_limit_bytes=48 * 1024 * 1024
        ),
        name="tide",
    )(
        elevation.reshape(flat), east_velocity.reshape(flat), north_velocity.reshape(flat),
        water_depth, land_sea,
    )
    shape = (members, rows, cols)
    return (h.reshape(shape), u.reshape(shape), v.reshape(shape), loading.reshape(members, rb_own, cb_own))


def solution(mesh):
    nx, ny = mesh.shape["gx"], mesh.shape["gy"]
    tile = P(None, "gy", "gx")
    return jax.shard_map(
        functools.partial(shards, nx, ny),
        mesh=mesh,
        in_specs=(tile, tile, tile, P("gy", "gx"), P("gy", "gx")),
        out_specs=(tile, tile, tile, tile),
        check_vma=False,
    )
```

time: 278 us -> 37.7 us (0.14)
  waiting for transfers between devices: 116 us -> 0 us
  starting transfers between devices: 106 us -> 0 us
  Pallas kernels: 0 us -> 29.9 us
  blocking collectives: 20 us -> 0 us
  between operations: 14.8 us -> 0.65 us
  other arithmetic: 9.35 us -> 0 us
  local copies, waits for them, and re-layouts: 9.84 us -> 6.79 us
    ppermute x64 -> x0, starting transfers between devices: 105 us -> none  [the longest x32 64.3 us: with_halo(): after = lax.ppermute(initial, axis, down)]
    ppermute x64 -> x0, waiting for transfers between devices: 78.6 us -> none  [the longest x32 52.2 us: with_halo(): before = lax.ppermute(last, axis, up)]
    reduce_scatter x2 -> x0, waiting for transfers between devices: 37.6 us -> none  [shards(): lax.psum_scatter(partial_value.reshape(members, coarse_rows, cols_here),...]
    pallas_call x0 -> x1, Pallas kernels: none -> 29.9 us  [shards(): pl.pallas_call(functools.partial(kernel, nx, ny, members, rows, cols), ou...]
    all_gather x2 -> x0, blocking collectives: 20 us -> none  [shards(): shard_piece = lax.all_gather(block_loads, 'gx', axis=1, tiled=True)]
    unnamed x14 -> x13, local copies, waits for them, and re-layouts: 0.22 us -> 6.1 us
    reshape x8 -> x1, local copies, waits for them, and re-layouts: 5.83 us -> 0.68 us  [shards(): loading.reshape(members, rb_own, cb_own)]
    mul x15 -> x0, other arithmetic: 3.48 us -> none  [the longest x8 2.16 us: shards(): east_rim = with_halo(water_depth * east_next, (('gx', 2),), 1, True)]
  transfers between devices with their start and end apart: 66 -> 0, of which waited for: 34 -> 0; matrix products, arithmetic and copies ran while one was open for 0% -> 0% of each run, Pallas kernels for 0% -> 0%
where the time goes in v1:
time: 37.7 us; the launch traced here: 37.3 us
  Pallas kernels  29.9 us (79%)
  local copies, waits for them, and re-layouts  6.79 us (18%)
  between operations  0.65 us (2%)
    pallas_call x1, Pallas kernels, shards(): pl.pallas_call(functools.partial(kernel, nx, ny, members, rows, cols), ou...  29.9 us
    unnamed x13, local copies, waits for them, and re-layouts  6.1 us

profile of v1, /device:TPU:0, one launch (start us, length us, event | category | flops | bytes accessed | tf_op | source)
XLA Modules:
  0.0 37.3 jit_solution(12936157451722736517)
XLA Ops:
  0.6 0.0 copy-start
  0.6 0.9 %copy-done = f32[8,32,128]{2,1,0:T(8,128)S(1)} copy-done((f32[8,32,128]{2,1,0:T(8,128)S(1)}, f32[8,32,128]{2,1,0:T(8,128)}, u32[]{:S(2)}) %copy-start) | copy-done | bytes 131096
  1.5 0.0 copy-start.1
  1.5 0.9 %copy-done.1 = f32[8,32,128]{2,1,0:T(8,128)S(1)} copy-done((f32[8,32,128]{2,1,0:T(8,128)S(1)}, f32[8,32,128]{2,1,0:T(8,128)}, u32[]{:S(2)}) %copy-start.1) | copy-done | bytes 131096
  2.4 0.0 copy-start.2
  2.4 0.9 %copy-done.2 = f32[8,32,128]{2,1,0:T(8,128)S(1)} copy-done((f32[8,32,128]{2,1,0:T(8,128)S(1)}, f32[8,32,128]{2,1,0:T(8,128)}, u32[]{:S(2)}) %copy-start.2) | copy-done | bytes 131096
  3.3 0.0 copy-start.3
  3.3 0.7 %copy-done.3 = f32[32,128]{1,0:T(8,128)S(1)} copy-done((f32[32,128]{1,0:T(8,128)S(1)}, f32[32,128]{1,0:T(8,128)}, u32[]{:S(2)}) %copy-start.3) | copy-done | bytes 16408
  4.1 0.0 copy-start.4
  4.1 0.7 %copy-done.4 = s32[32,128]{1,0:T(8,128)S(1)} copy-done((s32[32,128]{1,0:T(8,128)S(1)}, s32[32,128]{1,0:T(8,128)}, u32[]{:S(2)}) %copy-start.4) | copy-done | bytes 16408
  4.8 29.9 %tide.1 = (f32[256,128]{1,0:T(8,128)S(1)}, f32[256,128]{1,0:T(8,128)S(1)}, f32[256,128]{1,0:T(8,128)S(1)}, f32[8,64]{1,0:T(8,128)S(1)}) custom-call(f32[256,128]{1,0:T(8,128)S(1)} %bitcast.6, f32[256,128]{1,0:T(8,128)S(1)} %bitcast.7, f32[256,128]{1,0:T(8,128)S(1)} %bitcast.8, f32[32,128]{1,0:T(8,128)S(1)} %copy-done.3, s32[32,128]{1,0:T(8,128)S(1)} %copy-done.4), custom_call_target="tpu_custom_call" | custom-call | tf_op jit(solution)/shard_map/tide/pallas_call | solution.py:405
  34.7 0.7 %reshape.35 = f32[8,4,16]{2,1,0:T(4,128)} reshape(f32[8,64]{1,0:T(8,128)S(1)} %get-tuple-element.11) | data formatting | bytes 4096 | tf_op jit(solution)/shard_map/reshape | solution.py:448
  35.4 0.7 %copy.12 = f32[8,32,128]{2,1,0:T(8,128)} copy(f32[8,32,128]{2,1,0:T(8,128)S(1)} %bitcast.11) | data formatting | bytes 262144
  36.0 0.7 %copy.13 = f32[8,32,128]{2,1,0:T(8,128)} copy(f32[8,32,128]{2,1,0:T(8,128)S(1)} %bitcast.10) | data formatting | bytes 262144
  36.7 0.7 %copy.14 = f32[8,32,128]{2,1,0:T(8,128)} copy(f32[8,32,128]{2,1,0:T(8,128)S(1)} %bitcast.9) | data formatting | bytes 262144
Async XLA Ops:
  0.6 0.9 %copy-start = (f32[8,32,128]{2,1,0:T(8,128)S(1)}, f32[8,32,128]{2,1,0:T(8,128)}, u32[]{:S(2)}) copy-start(f32[8,32,128]{2,1,0:T(8,128)} %param.5) | copy-start | bytes 393220
  1.5 0.9 %copy-start.1 = (f32[8,32,128]{2,1,0:T(8,128)S(1)}, f32[8,32,128]{2,1,0:T(8,128)}, u32[]{:S(2)}) copy-start(f32[8,32,128]{2,1,0:T(8,128)} %param.6) | copy-start | bytes 393220
  2.4 0.9 %copy-start.2 = (f32[8,32,128]{2,1,0:T(8,128)S(1)}, f32[8,32,128]{2,1,0:T(8,128)}, u32[]{:S(2)}) copy-start(f32[8,32,128]{2,1,0:T(8,128)} %param.7) | copy-start | bytes 393220
  3.3 0.7 %copy-start.3 = (f32[32,128]{1,0:T(8,128)S(1)}, f32[32,128]{1,0:T(8,128)}, u32[]{:S(2)}) copy-start(f32[32,128]{1,0:T(8,128)} %d_in.1) | copy-start | bytes 49156
  4.1 0.7 %copy-start.4 = (s32[32,128]{1,0:T(8,128)S(1)}, s32[32,128]{1,0:T(8,128)}, u32[]{:S(2)}) copy-start(s32[32,128]{1,0:T(8,128)} %o_in.1) | copy-start | bytes 49156

commit v2 on v1

--- a/solution.py
+++ b/solution.py
@@ -58,8 +58,8 @@
 def kernel(
     nx, ny, members, rows, cols,
     h_in, u_in, v_in, d_in, o_in,
-    h_out, u_out, v_out, l_out,
-    in3, in_d, in_o, own, strips, land, slab, st, st_land, st_ns, dmx, turn,
+    own, l_out,
+    in3, in_d, in_o, strips, land, slab, st, st_land, st_ns, dmx, turn,
     eta, uu, vv, green, tiles, fine, ind, expand,
     in_sem, gs_sem, gr_sem, hs_sem, hr_sem, ss_sem, sr_sem,
 ):
@@ -83,21 +83,30 @@
     for copy in inputs:
         copy.start()
 
-    def partner(offset):
-        slot = lax.rem(my_slot + offset, n)
-        pair = slot // 2
-        return {"gx": (pair // ny) * 2 + slot % 2, "gy": pair % ny}
+    def wrap(index, size):
+        return jnp.where(index >= size, index - size, index)
+
+    def to_all_others(fn):
+        others = [wrap(gy + dy, ny) for dy in range(ny)]
+        for y in others[1:]:
+            fn({"gx": gx, "gy": y})
+
+        def column(dx, carry):
+            x = wrap(gx + dx, nx)
+            for y in others:
+                fn({"gx": x, "gy": y})
+            return carry
+
+        lax.fori_loop(1, nx, column, 0)
 
     barrier = pltpu.get_barrier_semaphore()
 
-    def greet(offset, carry):
-        pl.semaphore_signal(barrier, inc=1, device_id=partner(offset), device_id_type=MESH)
-        return carry
-
-    lax.fori_loop(1, n, greet, 0)
+    to_all_others(
+        lambda device: pl.semaphore_signal(barrier, inc=1, device_id=device, device_id_type=MESH)
+    )
 
     def target_of(dx, dy):
-        return {"gx": lax.rem(gx + dx + nx, nx), "gy": gy + dy}
+        return {"gx": wrap(jnp.where(gx + dx < 0, gx + dx + nx, gx + dx), nx), "gy": gy + dy}
 
     def when(dy, sending, fn):
         if dy == 0:
@@ -158,9 +167,25 @@
         for f in range(3):
             own[f, k] = in3[f, pl.ds(k, members, stride=rows), :]
 
-    pl.semaphore_wait(barrier, n - 1)
-    for k, (dx, dy) in enumerate(DIRS):
-        when(dy, True, lambda k=k: static_copy(k).start())
+    def early_setup():
+        north = per_device
+        south = north + cb_own
+        west = south + cb_own
+        east = west + rb_own + 2
+        t_id = iota((128, 2 * cols), 0)
+        l_id = iota((128, 2 * cols), 1)
+        for e in range(ext_tiles):
+            base = north if e == 0 else south if e == ext_tiles - 1 else (e - 1) * cb_own
+            want = jnp.where(
+                l_id < cols, base + l_id // BLOCK, jnp.where(l_id < cols + cols // 2, east + e, west + e)
+            )
+            expand[:, e * 2 * cols : (e + 1) * 2 * cols] = jnp.where(want == t_id, 1.0, 0.0).astype(BF16)
+
+        for e in range(ext_tiles):
+            row_ids = gy * rows - HALO + e * BLOCK + iota((BLOCK, cols), 0)
+            turning = CORIOLIS * jnp.sin(latitude(row_ids, rows * ny))
+            for k in range(BLOCK):
+                turn[e * BLOCK + k] = jnp.broadcast_to(turning[k : k + 1], (members, cols))
 
     def setup():
         t = iota((8, 128), 1)
@@ -196,21 +221,6 @@
             return carry
 
         lax.fori_loop(0, n // 16, green_group, 0)
-
-        t_id = iota((128, 2 * cols), 0)
-        l_id = iota((128, 2 * cols), 1)
-        for e in range(ext_tiles):
-            base = north if e == 0 else south if e == ext_tiles - 1 else (e - 1) * cb_own
-            want = jnp.where(
-                l_id < cols, base + l_id // BLOCK, jnp.where(l_id < cols + cols // 2, east + e, west + e)
-            )
-            expand[:, e * 2 * cols : (e + 1) * 2 * cols] = jnp.where(want == t_id, 1.0, 0.0).astype(BF16)
-
-        for e in range(ext_tiles):
-            row_ids = gy * rows - HALO + e * BLOCK + iota((BLOCK, cols), 0)
-            turning = CORIOLIS * jnp.sin(latitude(row_ids, rows * ny))
-            for k in range(BLOCK):
-                turn[e * BLOCK + k] = jnp.broadcast_to(turning[k : k + 1], (members, cols))
 
         for k, (dx, dy) in enumerate(DIRS):
             when(dy, False, lambda k=k: static_copy(k).wait_recv())
@@ -285,7 +295,7 @@
         carry = lax.fori_loop(0, full, lambda c, x: chunk(start + c * CHUNK, CHUNK, x), carry)
         chunk(start + full * CHUNK, count - full * CHUNK, carry)
 
-    def interval(i, _):
+    def begin(i):
         sums = []
         for b in range(rb_own):
             total = None
@@ -298,21 +308,6 @@
         loads = exact_dot(jnp.concatenate(sums, axis=1), ind[...]) / BLOCK
         tiles[i, my_slot] = loads.astype(BF16)
 
-        def gather_copy(offset):
-            return pltpu.make_async_remote_copy(
-                src_ref=tiles.at[i, my_slot], dst_ref=tiles.at[i, my_slot],
-                send_sem=gs_sem.at[i], recv_sem=gr_sem.at[i],
-                device_id=partner(offset), device_id_type=MESH,
-            )
-
-        def send(offset, carry):
-            gather_copy(offset).start()
-            return carry
-
-        lax.fori_loop(1, n, send, 0)
-        for k in (0, 1):
-            when(DIRS[k][1], True, lambda k=k: halo_copy(i, k).start())
-
         for f in range(3):
             for b in range(rb_own):
                 packed = None
@@ -320,7 +315,17 @@
                     moved = pltpu.roll(own[f, b * BLOCK + k], (HALO + 2 * HALO * k) % cols, 1)
                     packed = moved if packed is None else jnp.where(lane // (2 * HALO) == k, moved, packed)
                 strips[i, f, b] = packed
-        for k in range(2, len(DIRS)):
+
+    def interval(i, _):
+        def send(device):
+            pltpu.make_async_remote_copy(
+                src_ref=tiles.at[i, my_slot], dst_ref=tiles.at[i, my_slot],
+                send_sem=gs_sem.at[i], recv_sem=gr_sem.at[i],
+                device_id=device, device_id_type=MESH,
+            ).start()
+
+        to_all_others(send)
+        for k in range(len(DIRS)):
             when(DIRS[k][1], True, lambda k=k: halo_copy(i, k).start())
 
         pl.when(i == 0)(setup)
@@ -328,7 +333,7 @@
         everyone = pltpu.make_async_remote_copy(
             src_ref=tiles.at[i, pl.ds(0, n - 1)], dst_ref=tiles.at[i, pl.ds(0, n - 1)],
             send_sem=gs_sem.at[i], recv_sem=gr_sem.at[i],
-            device_id=partner(1), device_id_type=MESH,
+            device_id=target_of(1, 0), device_id_type=MESH,
         )
         everyone.wait_recv()
 
@@ -383,12 +388,32 @@
             own[0, r] = eta[last, HALO + r, :, :cols] + fine[1 + r // BLOCK, :, :cols]
             own[1, r] = uu[last, HALO + r, :, :cols]
             own[2, r] = vv[last, HALO + r, :, :cols]
+        pl.when(i < INTERVALS - 1)(lambda: begin(i + 1))
         return 0
 
+    begin(0)
+    early_setup()
+    pl.semaphore_wait(barrier, n - 1)
+    for k, (dx, dy) in enumerate(DIRS):
+        when(dy, True, lambda k=k: static_copy(k).start())
     lax.fori_loop(0, INTERVALS, interval, 0)
-    for r in range(rows):
-        for f, out in enumerate((h_out, u_out, v_out)):
-            out[pl.ds(r, members, stride=rows), :] = own[f, r]
+
+
+def place_outputs(members, rows, own, l_in, h_out, u_out, v_out, l_out, staged, l_staged, sem):
+    copies = [
+        pltpu.make_async_copy(staged.at[f], out, sem.at[f]) for f, out in enumerate((h_out, u_out, v_out))
+    ]
+    for f in range(3):
+        for r in range(rows):
+            staged[f, pl.ds(r, members, stride=rows), :] = own[f, r]
+        copies[f].start()
+    blocks, width = l_staged.shape[1:]
+    for b in range(blocks):
+        l_staged[:, b, :] = l_in[:, b * width : (b + 1) * width]
+    copies.append(pltpu.make_async_copy(l_staged, l_out, sem.at[3]))
+    copies[3].start()
+    for copy in copies:
+        copy.wait()
 
 
 def shards(nx, ny, elevation, east_velocity, north_velocity, water_depth, land_sea):
@@ -398,20 +423,22 @@
     ext = rows + 2 * HALO
     tiles = ext // BLOCK
     flat = (members * rows, cols)
-    any_spec = pl.BlockSpec(memory_space=pl.ANY)
+    hbm_spec = pl.BlockSpec(memory_space=pltpu.HBM)
     vmem_spec = pl.BlockSpec(memory_space=pltpu.VMEM)
     dma = pltpu.SemaphoreType.DMA
     field = jax.ShapeDtypeStruct(flat, F32)
-    h, u, v, loading = pl.pallas_call(
+    own, loading = pl.pallas_call(
         functools.partial(kernel, nx, ny, members, rows, cols),
-        out_shape=(field, field, field, jax.ShapeDtypeStruct((members, rb_own * cb_own), F32)),
-        in_specs=[any_spec] * 5,
-        out_specs=(vmem_spec,) * 4,
+        out_shape=(
+            jax.ShapeDtypeStruct((3, rows, members, cols), F32),
+            jax.ShapeDtypeStruct((members, rb_own * cb_own), F32),
+        ),
+        in_specs=[hbm_spec] * 5,
+        out_specs=(vmem_spec,) * 2,
         scratch_shapes=[
             pltpu.VMEM((3,) + flat, F32),
             pltpu.VMEM((rows, cols), F32),
             pltpu.VMEM((rows, cols), jnp.int32),
-            pltpu.VMEM((3, rows, members, cols), F32),
             pltpu.VMEM((INTERVALS, 3, rb_own, members, cols), F32),
             pltpu.VMEM((INTERVALS, 2, 3, tiles, members, cols), F32),
             pltpu.VMEM((INTERVALS, 2, 3, HALO, members, cols), F32),
@@ -441,11 +468,26 @@
         ),
         name="tide",
     )(
-        elevation.reshape(flat), east_velocity.reshape(flat), north_velocity.reshape(flat),
-        water_depth, land_sea,
+        *(
+            pltpu.with_memory_space_constraint(x, pltpu.HBM)
+            for x in (
+                elevation.reshape(flat), east_velocity.reshape(flat), north_velocity.reshape(flat),
+                water_depth, land_sea,
+            )
+        )
     )
+    coarse = jax.ShapeDtypeStruct((members, rb_own, cb_own), F32)
+    h, u, v, loading = pl.pallas_call(
+        functools.partial(place_outputs, members, rows),
+        out_shape=(field, field, field, coarse),
+        in_specs=[vmem_spec] * 2,
+        out_specs=(hbm_spec,) * 4,
+        scratch_shapes=[pltpu.VMEM((3,) + flat, F32), pltpu.VMEM(coarse.shape, F32), dma((4,))],
+        compiler_params=pltpu.CompilerParams(vmem_limit_bytes=4 * 1024 * 1024),
+        name="place",
+    )(own, loading)
     shape = (members, rows, cols)
-    return (h.reshape(shape), u.reshape(shape), v.reshape(shape), loading.reshape(members, rb_own, cb_own))
+    return (h.reshape(shape), u.reshape(shape), v.reshape(shape), loading)
 
 
 def solution(mesh):

time: 37.7 us -> 29.8 us (0.79)
  local copies, waits for them, and re-layouts: 6.79 us -> 0 us
  Pallas kernels: 29.9 us -> 29 us
    unnamed x13 -> x0, local copies, waits for them, and re-layouts: 6.1 us -> none
    pallas_call x1, Pallas kernels: 29.9 us -> 28.1 us  [shards(): pl.pallas_call(functools.partial(kernel, nx, ny, members, rows, cols), ou...]
    pallas_call x0 -> x1, Pallas kernels: none -> 0.93 us  [shards(): pl.pallas_call(functools.partial(place_outputs, members, rows), out_shape...]
    reshape x1 -> x0, local copies, waits for them, and re-layouts: 0.68 us -> none  [shards(): loading.reshape(members, rb_own, cb_own)]
where the time goes in v2:
time: 29.8 us; the launch traced here: 29.7 us
  Pallas kernels  29 us (97%)
  between operations  0.64 us (2%)
    pallas_call x1, Pallas kernels, shards(): pl.pallas_call(functools.partial(kernel, nx, ny, members, rows, cols), ou...  28.1 us
    pallas_call x1, Pallas kernels, shards(): pl.pallas_call(functools.partial(place_outputs, members, rows), out_shape...  0.93 us

profile of v2, /device:TPU:0, one launch (start us, length us, event | category | flops | bytes accessed | tf_op | source)
XLA Modules:
  0.0 29.7 jit_solution(7324957551347055298)
XLA Ops:
  0.6 28.1 %tide.1 = (f32[3,32,8,128]{3,2,1,0:T(8,128)S(1)}, f32[8,64]{1,0:T(8,128)S(1)}) custom-call(f32[256,128]{1,0:T(8,128)} %bitcast.6, f32[256,128]{1,0:T(8,128)} %bitcast.7, f32[256,128]{1,0:T(8,128)} %bitcast.8, f32[32,128]{1,0:T(8,128)} %d_in.1, s32[32,128]{1,0:T(8,128)} %o_in.1), custom_call_target="tpu_custom_call" | custom-call | tf_op jit(solution)/shard_map/tide/pallas_call | solution.py:430
  28.8 0.9 %place.1 = (f32[256,128]{1,0:T(8,128)}, f32[256,128]{1,0:T(8,128)}, f32[256,128]{1,0:T(8,128)}, f32[8,4,16]{2,1,0:T(4,128)}) custom-call(f32[3,32,8,128]{3,2,1,0:T(8,128)S(1)} %get-tuple-element.10.own, f32[8,64]{1,0:T(8,128)S(1)} %get-tuple-element.11.l_in), custom_call_target="tpu_custom_call" | custom-call | tf_op jit(solution)/shard_map/place/pallas_call | solution.py:480

commit v3 on v2

--- a/solution.py
+++ b/solution.py
@@ -73,6 +73,7 @@
     ext_tiles = ext // BLOCK
     my_slot = ((gx // 2) * ny + gy) * 2 + gx % 2
     lane = iota((members, cols), 1)
+    half = 0.5 * COURANT
 
     inputs = [
         pltpu.make_async_copy(src, dst, in_sem.at[k])
@@ -234,6 +235,7 @@
                 main = st[(e - 1) * BLOCK : e * BLOCK]
             part = slice(e * BLOCK, (e + 1) * BLOCK)
             side = jnp.where(iota((BLOCK, cols), 1) < cols // 2, st_land[1, part], st_land[0, part])
+            main, side = main * (half * half), side * (half * half)
             for k in range(BLOCK):
                 dmx[e * BLOCK + k, :, :cols] = jnp.broadcast_to(main[k : k + 1], (members, cols))
                 dmx[e * BLOCK + k, :, cols:] = jnp.broadcast_to(side[k : k + 1], (members, cols))
@@ -247,7 +249,6 @@
             jnp.where(at_end, rm, ra) - jnp.where(at_start, lm, la),
         )
 
-    half = 0.5 * COURANT
     keep = 1.0 - FRICTION
 
     def sweep(step):
@@ -268,8 +269,8 @@
             for c in range(2):
                 part = slice(c * cols, (c + 1) * cols)
                 wet = depth[c] > 0.0
-                u_next = keep * u_now[c] + coriolis * v_now[c] - half * grad[c]
-                v_next = keep * v_now[c] - coriolis * u_now[c] - half * (after[c] - before[c])
+                u_next = keep * u_now[c] + coriolis * v_now[c] - grad[c]
+                v_next = keep * v_now[c] - coriolis * u_now[c] - (after[c] - before[c])
                 u_next = jnp.where(wet, u_next, 0.0)
                 v_next = jnp.where(wet, v_next, 0.0)
                 uu[dst, r, :, part] = u_next
@@ -279,7 +280,7 @@
             flow = xdiff(*du)
             for c in range(2):
                 part = slice(c * cols, (c + 1) * cols)
-                out = half * (flow_one[c] + (dv[c] - north_two[c]))
+                out = flow_one[c] + (dv[c] - north_two[c])
                 eta[dst, r - 1, :, part] = jnp.where(depth_one[c] > 0.0, before[c] - out, before[c])
             return here, after, north_one, tuple(dv), flow
 
@@ -327,6 +328,10 @@
         to_all_others(send)
         for k in range(len(DIRS)):
             when(DIRS[k][1], True, lambda k=k: halo_copy(i, k).start())
+
+        for r in range(rows):
+            uu[0, HALO + r, :, :cols] = own[1, r]
+            vv[0, HALO + r, :, :cols] = own[2, r]
 
         pl.when(i == 0)(setup)
 
@@ -376,16 +381,17 @@
                         main = own[f, r - HALO]
                     side = pltpu.roll(joined, (-(2 * HALO * k + HALO)) % cols, 1)
                     if f == 0:
-                        main = main - fine[e, :, :cols]
-                        side = side - fine[e, :, cols:]
-                    ref[0, r, :, :cols] = main
+                        main = half * (main - fine[e, :, :cols])
+                        side = half * (side - fine[e, :, cols:])
+                    if f == 0 or e in (0, ext_tiles - 1):
+                        ref[0, r, :, :cols] = main
                     ref[0, r, :, cols:] = side
 
         for step in range(STEPS):
             sweep(step)
         last = STEPS % 2
         for r in range(rows):
-            own[0, r] = eta[last, HALO + r, :, :cols] + fine[1 + r // BLOCK, :, :cols]
+            own[0, r] = eta[last, HALO + r, :, :cols] * (1.0 / half) + fine[1 + r // BLOCK, :, :cols]
             own[1, r] = uu[last, HALO + r, :, :cols]
             own[2, r] = vv[last, HALO + r, :, :cols]
         pl.when(i < INTERVALS - 1)(lambda: begin(i + 1))

time: 29.8 us -> 29.9 us (level)
  no operation moved by 1% of the time
where the time goes in v3:
time: 29.9 us; the launch traced here: 29.8 us
  Pallas kernels  29.1 us (97%)
  between operations  0.64 us (2%)
    pallas_call x1, Pallas kernels, shards(): pl.pallas_call(functools.partial(kernel, nx, ny, members, rows, cols), ou...  28.2 us
    pallas_call x1, Pallas kernels, shards(): pl.pallas_call(functools.partial(place_outputs, members, rows), out_shape...  0.93 us

profile of v3, /device:TPU:0, one launch (start us, length us, event | category | flops | bytes accessed | tf_op | source)
XLA Modules:
  0.0 29.8 jit_solution(4215799042290080193)
XLA Ops:
  0.6 28.2 %tide.1 = (f32[3,32,8,128]{3,2,1,0:T(8,128)S(1)}, f32[8,64]{1,0:T(8,128)S(1)}) custom-call(f32[256,128]{1,0:T(8,128)} %bitcast.6, f32[256,128]{1,0:T(8,128)} %bitcast.7, f32[256,128]{1,0:T(8,128)} %bitcast.8, f32[32,128]{1,0:T(8,128)} %d_in.1, s32[32,128]{1,0:T(8,128)} %o_in.1), custom_call_target="tpu_custom_call" | custom-call | tf_op jit(solution)/shard_map/tide/pallas_call | solution.py:436
  28.9 0.9 %place.1 = (f32[256,128]{1,0:T(8,128)}, f32[256,128]{1,0:T(8,128)}, f32[256,128]{1,0:T(8,128)}, f32[8,4,16]{2,1,0:T(4,128)}) custom-call(f32[3,32,8,128]{3,2,1,0:T(8,128)S(1)} %get-tuple-element.10.own, f32[8,64]{1,0:T(8,128)S(1)} %get-tuple-element.11.l_in), custom_call_target="tpu_custom_call" | custom-call | tf_op jit(solution)/shard_map/place/pallas_call | solution.py:486

commit v4 on v3

--- a/solution.py
+++ b/solution.py
@@ -59,7 +59,7 @@
     nx, ny, members, rows, cols,
     h_in, u_in, v_in, d_in, o_in,
     own, l_out,
-    in3, in_d, in_o, strips, land, slab, st, st_land, st_ns, dmx, turn,
+    in3, in_d, in_o, strips, land, slab_out, slab, st, st_land, st_ns, dmx, turn,
     eta, uu, vv, green, tiles, fine, ind, expand,
     in_sem, gs_sem, gr_sem, hs_sem, hr_sem, ss_sem, sr_sem,
 ):
@@ -134,8 +134,8 @@
         dx, dy = DIRS[k]
         side = 0 if dx > 0 else 1
         if dx == 0:
-            src = own.at[:, pl.ds(rows - HALO if dy > 0 else 0, HALO)]
-            dst = slab.at[i, 0 if dy > 0 else 1]
+            at = 0 if dy > 0 else 1
+            src, dst = slab_out.at[i, at], slab.at[i, at]
         elif dy == 0:
             src, dst = strips.at[i], land.at[i, side, :, pl.ds(1, rb_own)]
         else:
@@ -309,6 +309,13 @@
         loads = exact_dot(jnp.concatenate(sums, axis=1), ind[...]) / BLOCK
         tiles[i, my_slot] = loads.astype(BF16)
 
+        for at, first in enumerate((rows - HALO, 0)):
+            for f in range(3):
+                for k in range(HALO // 2):
+                    r = first + 2 * k
+                    both = jnp.concatenate([own[f, r], own[f, r + 1]], axis=0)
+                    slab_out[i, at, f, k] = both.astype(BF16)
+
         for f in range(3):
             for b in range(rb_own):
                 packed = None
@@ -368,15 +375,19 @@
         for k, (dx, dy) in enumerate(DIRS):
             when(dy, True, lambda k=k: halo_copy(i, k).wait_send())
 
+        def edge_row(at, f, k):
+            part = slice(k % 2 * members, (k % 2 + 1) * members)
+            return slab[i, at, f, k // 2].astype(F32)[part]
+
         for f, ref in enumerate((eta, uu, vv)):
             for e in range(ext_tiles):
                 joined = jnp.where(lane % (2 * HALO) < HALO, land[i, 0, f, e], land[i, 1, f, e])
                 for k in range(BLOCK):
                     r = e * BLOCK + k
                     if e == 0:
-                        main = slab[i, 0, f, k]
+                        main = edge_row(0, f, k)
                     elif e == ext_tiles - 1:
-                        main = slab[i, 1, f, k]
+                        main = edge_row(1, f, k)
                     else:
                         main = own[f, r - HALO]
                     side = pltpu.roll(joined, (-(2 * HALO * k + HALO)) % cols, 1)
@@ -447,7 +458,8 @@
             pltpu.VMEM((rows, cols), jnp.int32),
             pltpu.VMEM((INTERVALS, 3, rb_own, members, cols), F32),
             pltpu.VMEM((INTERVALS, 2, 3, tiles, members, cols), F32),
-            pltpu.VMEM((INTERVALS, 2, 3, HALO, members, cols), F32),
+            pltpu.VMEM((INTERVALS, 2, 3, HALO // 2, 2 * members, cols), BF16),
+            pltpu.VMEM((INTERVALS, 2, 3, HALO // 2, 2 * members, cols), BF16),
             pltpu.VMEM((rows, cols), F32),
             pltpu.VMEM((2, ext, cols), F32),
             pltpu.VMEM((2, HALO, cols), F32),

time: 29.9 us -> 28.7 us (0.960)
  Pallas kernels: 29.1 us -> 27.9 us
    pallas_call x1, Pallas kernels: 28.2 us -> 27 us  [shards(): pl.pallas_call(functools.partial(kernel, nx, ny, members, rows, cols), ou...]
where the time goes in v4:
time: 28.7 us; the launch traced here: 28.6 us
  Pallas kernels  27.9 us (97%)
  between operations  0.64 us (2%)
    pallas_call x1, Pallas kernels, shards(): pl.pallas_call(functools.partial(kernel, nx, ny, members, rows, cols), ou...  27 us
    pallas_call x1, Pallas kernels, shards(): pl.pallas_call(functools.partial(place_outputs, members, rows), out_shape...  0.93 us

profile of v4, /device:TPU:0, one launch (start us, length us, event | category | flops | bytes accessed | tf_op | source)
XLA Modules:
  0.0 28.6 jit_solution(13926113082677582643)
XLA Ops:
  0.6 27.0 %tide.1 = (f32[3,32,8,128]{3,2,1,0:T(8,128)S(1)}, f32[8,64]{1,0:T(8,128)S(1)}) custom-call(f32[256,128]{1,0:T(8,128)} %bitcast.6, f32[256,128]{1,0:T(8,128)} %bitcast.7, f32[256,128]{1,0:T(8,128)} %bitcast.8, f32[32,128]{1,0:T(8,128)} %d_in.1, s32[32,128]{1,0:T(8,128)} %o_in.1), custom_call_target="tpu_custom_call" | custom-call | tf_op jit(solution)/shard_map/tide/pallas_call | solution.py:447
  27.7 0.9 %place.1 = (f32[256,128]{1,0:T(8,128)}, f32[256,128]{1,0:T(8,128)}, f32[256,128]{1,0:T(8,128)}, f32[8,4,16]{2,1,0:T(4,128)}) custom-call(f32[3,32,8,128]{3,2,1,0:T(8,128)S(1)} %get-tuple-element.10.own, f32[8,64]{1,0:T(8,128)S(1)} %get-tuple-element.11.l_in), custom_call_target="tpu_custom_call" | custom-call | tf_op jit(solution)/shard_map/place/pallas_call | solution.py:498
